TPU v7x, 32 devices: a whole 2x2x4 slice. The times are simulated.
32 devices in a mesh: row: 2 (over y), col: 16 (over z, x, core).
Axes of the slice: x: 2, y: 2, z: 4, core: 2. Of those that a mesh axis runs over, the one named last changes fastest.
Arguments:
- tokens: bfloat16 [25088, 1024], P(('col', 'row')), may hold values from -6 to 6
- w_qkv: bfloat16 [1024, 3072], P('row', 'col'), may hold values from -0.1875 to 0.1875
- w_proj: bfloat16 [1024, 1024], P('row', 'col'), may hold values from -6 to 6
- w_fc1: bfloat16 [1024, 4096], P('row', 'col'), may hold values from -0.1875 to 0.1875
- w_fc2: bfloat16 [4096, 1024], P('row', 'col'), may hold values from -0.09375 to 0.09375
- ln1_gain: bfloat16 [1024], P(('col', 'row')), may hold values from 0.099609375 to 1.8984375
- ln1_bias: bfloat16 [1024], P(('col', 'row')), may hold values from -6 to 6
- q_bias: bfloat16 [1024], P(('col', 'row')), may hold values from -6 to 6
- v_bias: bfloat16 [1024], P(('col', 'row')), may hold values from -0.4375 to 0.4375
- proj_bias: bfloat16 [1024], P(('col', 'row')), may hold values from -6 to 6
- ln2_gain: bfloat16 [1024], P(('col', 'row')), may hold values from 0.099609375 to 1.8984375
- ln2_bias: bfloat16 [1024], P(('col', 'row')), may hold values from -6 to 6
- fc1_bias: bfloat16 [4096], P(('col', 'row')), may hold values from -6 to 6
- fc2_bias: bfloat16 [1024], P(('col', 'row')), may hold values from -6 to 6
- cotangent: float32 [25088, 1024], P(('col', 'row')), may hold values from -6 to 6
Outputs:
- output: bfloat16 [25088, 1024], P(('col', 'row'))
- grad_tokens: float32 [25088, 1024], P(('col', 'row'))
- grad_qkv: float32 [1024, 3072], P('row', 'col')
- grad_proj: float32 [1024, 1024], P('row', 'col')
- grad_fc1: float32 [1024, 4096], P('row', 'col')
- grad_fc2: float32 [4096, 1024], P('row', 'col')
- grad_ln1_gain: float32 [1024], P(('col', 'row'))
- grad_ln1_bias: float32 [1024], P(('col', 'row'))
- grad_q_bias: float32 [1024], P(('col', 'row'))
- grad_v_bias: float32 [1024], P(('col', 'row'))
- grad_proj_bias: float32 [1024], P(('col', 'row'))
- grad_ln2_gain: float32 [1024], P(('col', 'row'))
- grad_ln2_bias: float32 [1024], P(('col', 'row'))
- grad_fc1_bias: float32 [4096], P(('col', 'row'))
- grad_fc2_bias: float32 [1024], P(('col', 'row'))
All inputs are finite; a program needn't handle non-finite values.
Results may differ from a plain program's by a relative error of at most 0.019.
Values may be sent and summed in bfloat16 or wider, within the bound.
No kernel may reach another device: no remote copies, remote signals or barrier semaphores. Data moves between devices by JAX's collectives and lax.ppermute only.
A program may use at most 448 MiB of HBM per device.

v0:
```python
import math

import jax
import jax.numpy as jnp
from jax import lax
from jax.sharding import PartitionSpec as P

D = 1024
H = 16
HD = 64
LEN = 1568


EPSILON = 1e-06


def layer_norm(value, gain, shift):
    average = jnp.mean(value, axis=-1, keepdims=True)
    centred = value - average
    spread = jnp.mean(centred * centred, axis=-1, keepdims=True)
    inverse = lax.rsqrt(spread + EPSILON)
    normed = centred * inverse
    return (normed * gain + shift, normed, inverse)


def norm_back(grad_out, normed, inverse, gain):
    scaled = grad_out * gain
    mean_first = jnp.mean(scaled, axis=-1, keepdims=True)
    mean_second = jnp.mean(scaled * normed, axis=-1, keepdims=True)
    return inverse * (scaled - mean_first - normed * mean_second)


def gelu_slope(pre_act):
    cumulative = 0.5 * (1.0 + lax.erf(pre_act * 2.0 ** (-0.5)))
    density = jnp.exp(-0.5 * pre_act * pre_act) * (2.0 * math.pi) ** (-0.5)
    return cumulative + pre_act * density


def inner_rows(first, second):
    return lax.dot_general(
        first, second, (((0,), (0,)), ((), ())), preferred_element_type=jnp.float32
    )


def outer_cols(first, second):
    return lax.dot_general(
        first, second, (((1,), (1,)), ((), ())), preferred_element_type=jnp.float32
    )


def clip_forward(block):
    queries, key_rows, value_rows = (block[:, 0], block[:, 1], block[:, 2])
    scores = jnp.einsum(
        "qhd,khd->hqk", queries, key_rows, preferred_element_type=jnp.float32
    ) * HD ** (-0.5)
    row_peak = jnp.max(scores, axis=-1, keepdims=True)
    exponent = jnp.exp(scores - row_peak)
    row_total = jnp.sum(exponent, axis=-1, keepdims=True)
    weights_low = (exponent / row_total).astype(jnp.bfloat16)
    mixed_heads = jnp.einsum(
        "hqk,khd->qhd", weights_low, value_rows, preferred_element_type=jnp.float32
    )
    return (mixed_heads.astype(jnp.bfloat16), (row_peak + jnp.log(row_total))[..., 0])


def clip_backward(element):
    block, grad_mixed, logsum = element
    queries, key_rows, value_rows = (block[:, 0], block[:, 1], block[:, 2])
    scores = jnp.einsum(
        "qhd,khd->hqk", queries, key_rows, preferred_element_type=jnp.float32
    ) * HD ** (-0.5)
    weights_full = jnp.exp(scores - logsum[..., None])
    weights_low = weights_full.astype(jnp.bfloat16)
    grad_values = jnp.einsum(
        "hqk,qhd->khd", weights_low, grad_mixed, preferred_element_type=jnp.float32
    )
    grad_weights = jnp.einsum(
        "qhd,khd->hqk", grad_mixed, value_rows, preferred_element_type=jnp.float32
    )
    row_delta = jnp.sum(grad_weights * weights_full, axis=-1, keepdims=True)
    grad_scores = (weights_full * (grad_weights - row_delta)).astype(jnp.bfloat16)
    grad_queries = jnp.einsum(
        "hqk,khd->qhd", grad_scores, key_rows, preferred_element_type=jnp.float32
    ) * HD ** (-0.5)
    grad_keys = jnp.einsum(
        "hqk,qhd->khd", grad_scores, queries, preferred_element_type=jnp.float32
    ) * HD ** (-0.5)
    return jnp.stack([grad_queries, grad_keys, grad_values], axis=1).astype(jnp.bfloat16)


def per_device(
    tokens,
    w_qkv,
    w_proj,
    w_fc1,
    w_fc2,
    ln1_gain,
    ln1_bias,
    q_bias,
    v_bias,
    proj_bias,
    ln2_gain,
    ln2_bias,
    fc1_bias,
    fc2_bias,
    cotangent,
):
    (
        qkv_part,
        proj_part,
        fc1_part,
        fc2_part,
        gain1_part,
        shift1_part,
        biasq_part,
        biasv_part,
        biasp_part,
        gain2_part,
        shift2_part,
        bias1_part,
        bias2_part,
    ) = (
        lax.all_gather(w_qkv, "row", axis=0, tiled=True),
        lax.all_gather(w_proj, "row", axis=0, tiled=True),
        lax.all_gather(w_fc1, "row", axis=0, tiled=True),
        lax.all_gather(w_fc2, "row", axis=0, tiled=True),
        lax.all_gather(ln1_gain, "row", axis=0, tiled=True),
        lax.all_gather(ln1_bias, "row", axis=0, tiled=True),
        lax.all_gather(q_bias, "row", axis=0, tiled=True),
        lax.all_gather(v_bias, "row", axis=0, tiled=True),
        lax.all_gather(proj_bias, "row", axis=0, tiled=True),
        lax.all_gather(ln2_gain, "row", axis=0, tiled=True),
        lax.all_gather(ln2_bias, "row", axis=0, tiled=True),
        lax.all_gather(fc1_bias, "row", axis=0, tiled=True),
        lax.all_gather(fc2_bias, "row", axis=0, tiled=True),
    )
    (
        full_qkv,
        full_proj,
        full_fc1,
        full_fc2,
        full_gain1,
        full_shift1,
        full_biasq,
        full_biasv,
        full_biasp,
        full_gain2,
        full_shift2,
        full_bias1,
        full_bias2,
    ) = (
        lax.all_gather(qkv_part, "col", axis=1, tiled=True),
        lax.all_gather(proj_part, "col", axis=1, tiled=True),
        lax.all_gather(fc1_part, "col", axis=1, tiled=True),
        lax.all_gather(fc2_part, "col", axis=1, tiled=True),
        lax.all_gather(gain1_part, "col", axis=0, tiled=True),
        lax.all_gather(shift1_part, "col", axis=0, tiled=True),
        lax.all_gather(biasq_part, "col", axis=0, tiled=True),
        lax.all_gather(biasv_part, "col", axis=0, tiled=True),
        lax.all_gather(biasp_part, "col", axis=0, tiled=True),
        lax.all_gather(gain2_part, "col", axis=0, tiled=True),
        lax.all_gather(shift2_part, "col", axis=0, tiled=True),
        lax.all_gather(bias1_part, "col", axis=0, tiled=True),
        lax.all_gather(bias2_part, "col", axis=0, tiled=True),
    )
    gain_first = full_gain1.astype(jnp.float32)
    gain_second = full_gain2.astype(jnp.float32)
    groups = lax.axis_size("row")
    heads_local = H // groups
    per_group = heads_local * HD
    inputs = tokens.astype(jnp.float32)
    token_rows = inputs.shape[0]
    normed_out1, normed_one, inverse_one = layer_norm(
        inputs, gain_first, full_shift1.astype(jnp.float32)
    )
    hidden_one = normed_out1.astype(jnp.bfloat16)
    bias_q = full_biasq.astype(jnp.float32)
    qkv_bias = jnp.concatenate([bias_q, jnp.zeros_like(bias_q), full_biasv.astype(jnp.float32)])
    projected = jnp.dot(hidden_one, full_qkv, preferred_element_type=jnp.float32) + qkv_bias
    qkv_low = projected.astype(jnp.bfloat16).reshape(token_rows, 3, groups, per_group)
    by_heads = lax.all_to_all(qkv_low, "row", split_axis=2, concat_axis=0, tiled=True)
    col_rows = by_heads.shape[0]
    clip_count = col_rows // LEN
    blocks = by_heads.reshape(clip_count, LEN, 3, heads_local, HD)
    mixed_heads, logsum = lax.map(clip_forward, blocks)
    attended = lax.all_to_all(
        mixed_heads.reshape(col_rows, 1, per_group), "row", split_axis=0, concat_axis=1, tiled=True
    ).reshape(token_rows, D)
    middle = inputs + (
        jnp.dot(attended, full_proj, preferred_element_type=jnp.float32)
        + full_biasp.astype(jnp.float32)
    )
    normed_out2, normed_two, inverse_two = layer_norm(
        middle, gain_second, full_shift2.astype(jnp.float32)
    )
    hidden_two = normed_out2.astype(jnp.bfloat16)
    pre_act = jnp.dot(hidden_two, full_fc1, preferred_element_type=jnp.float32) + full_bias1.astype(
        jnp.float32
    )
    activated = jax.nn.gelu(pre_act, approximate=False).astype(jnp.bfloat16)
    result = middle + (
        jnp.dot(activated, full_fc2, preferred_element_type=jnp.float32)
        + full_bias2.astype(jnp.float32)
    )
    qkv_again, proj_again, fc1_again, fc2_again = (
        lax.all_gather(w_qkv, "row", axis=0, tiled=True),
        lax.all_gather(w_proj, "row", axis=0, tiled=True),
        lax.all_gather(w_fc1, "row", axis=0, tiled=True),
        lax.all_gather(w_fc2, "row", axis=0, tiled=True),
    )
    back_qkv, back_proj, back_fc1, back_fc2 = (
        lax.all_gather(qkv_again, "col", axis=1, tiled=True),
        lax.all_gather(proj_again, "col", axis=1, tiled=True),
        lax.all_gather(fc1_again, "col", axis=1, tiled=True),
        lax.all_gather(fc2_again, "col", axis=1, tiled=True),
    )
    grad_out = cotangent.astype(jnp.bfloat16)
    grad_bias2 = jnp.sum(grad_out.astype(jnp.float32), axis=0)
    grad_fc2 = inner_rows(activated, grad_out)
    grad_act = outer_cols(grad_out, back_fc2)
    grad_pre = (grad_act * gelu_slope(pre_act)).astype(jnp.bfloat16)
    grad_bias1 = jnp.sum(grad_pre.astype(jnp.float32), axis=0)
    grad_fc1 = inner_rows(hidden_two, grad_pre)
    grad_hidden2 = outer_cols(grad_pre, back_fc1)
    grad_gain2 = jnp.sum(grad_hidden2 * normed_two, axis=0)
    grad_shift2 = jnp.sum(grad_hidden2, axis=0)
    grad_middle = cotangent + norm_back(grad_hidden2, normed_two, inverse_two, gain_second)
    grad_branch = grad_middle.astype(jnp.bfloat16)
    grad_biasp = jnp.sum(grad_branch.astype(jnp.float32), axis=0)
    grad_proj = inner_rows(attended, grad_branch)
    grad_attended = outer_cols(grad_branch, back_proj).astype(jnp.bfloat16)
    grad_heads = lax.all_to_all(
        grad_attended.reshape(token_rows, groups, per_group),
        "row",
        split_axis=1,
        concat_axis=0,
        tiled=True,
    )
    grad_blocks = grad_heads.reshape(clip_count, LEN, heads_local, HD)
    grad_triple = lax.map(clip_backward, (blocks, grad_blocks, logsum))
    grad_tokens_qkv = lax.all_to_all(
        grad_triple.reshape(col_rows, 3, 1, per_group),
        "row",
        split_axis=0,
        concat_axis=2,
        tiled=True,
    ).reshape(token_rows, 3 * D)
    grad_qkv_float = grad_tokens_qkv.astype(jnp.float32)
    grad_biasq = jnp.sum(grad_qkv_float[:, :D], axis=0)
    grad_biasv = jnp.sum(grad_qkv_float[:, 2 * D :], axis=0)
    grad_qkv = inner_rows(hidden_one, grad_tokens_qkv)
    grad_hidden1 = outer_cols(grad_tokens_qkv, back_qkv)
    grad_gain1 = jnp.sum(grad_hidden1 * normed_one, axis=0)
    grad_shift1 = jnp.sum(grad_hidden1, axis=0)
    grad_inputs = grad_middle + norm_back(grad_hidden1, normed_one, inverse_one, gain_first)
    (
        sum_qkv,
        sum_proj,
        sum_fc1,
        sum_fc2,
        sum_gain1,
        sum_shift1,
        sum_biasq,
        sum_biasv,
        sum_biasp,
        sum_gain2,
        sum_shift2,
        sum_bias1,
        sum_bias2,
    ) = (
        lax.psum_scatter(
            grad_qkv.astype(jnp.bfloat16), "col", scatter_dimension=1, tiled=True
        ).astype(jnp.float32),
        lax.psum_scatter(
            grad_proj.astype(jnp.bfloat16), "col", scatter_dimension=1, tiled=True
        ).astype(jnp.float32),
        lax.psum_scatter(
            grad_fc1.astype(jnp.bfloat16), "col", scatter_dimension=1, tiled=True
        ).astype(jnp.float32),
        lax.psum_scatter(
            grad_fc2.astype(jnp.bfloat16), "col", scatter_dimension=1, tiled=True
        ).astype(jnp.float32),
        lax.psum_scatter(
            grad_gain1.astype(jnp.bfloat16), "col", scatter_dimension=0, tiled=True
        ).astype(jnp.float32),
        lax.psum_scatter(
            grad_shift1.astype(jnp.bfloat16), "col", scatter_dimension=0, tiled=True
        ).astype(jnp.float32),
        lax.psum_scatter(
            grad_biasq.astype(jnp.bfloat16), "col", scatter_dimension=0, tiled=True
        ).astype(jnp.float32),
        lax.psum_scatter(
            grad_biasv.astype(jnp.bfloat16), "col", scatter_dimension=0, tiled=True
        ).astype(jnp.float32),
        lax.psum_scatter(
            grad_biasp.astype(jnp.bfloat16), "col", scatter_dimension=0, tiled=True
        ).astype(jnp.float32),
        lax.psum_scatter(
            grad_gain2.astype(jnp.bfloat16), "col", scatter_dimension=0, tiled=True
        ).astype(jnp.float32),
        lax.psum_scatter(
            grad_shift2.astype(jnp.bfloat16), "col", scatter_dimension=0, tiled=True
        ).astype(jnp.float32),
        lax.psum_scatter(
            grad_bias1.astype(jnp.bfloat16), "col", scatter_dimension=0, tiled=True
        ).astype(jnp.float32),
        lax.psum_scatter(
            grad_bias2.astype(jnp.bfloat16), "col", scatter_dimension=0, tiled=True
        ).astype(jnp.float32),
    )
    (
        out_qkv,
        out_proj,
        out_fc1,
        out_fc2,
        out_gain1,
        out_shift1,
        out_biasq,
        out_biasv,
        out_biasp,
        out_gain2,
        out_shift2,
        out_bias1,
        out_bias2,
    ) = (
        lax.psum_scatter(
            sum_qkv.astype(jnp.bfloat16), "row", scatter_dimension=0, tiled=True
        ).astype(jnp.float32),
        lax.psum_scatter(
            sum_proj.astype(jnp.bfloat16), "row", scatter_dimension=0, tiled=True
        ).astype(jnp.float32),
        lax.psum_scatter(
            sum_fc1.astype(jnp.bfloat16), "row", scatter_dimension=0, tiled=True
        ).astype(jnp.float32),
        lax.psum_scatter(
            sum_fc2.astype(jnp.bfloat16), "row", scatter_dimension=0, tiled=True
        ).astype(jnp.float32),
        lax.psum_scatter(
            sum_gain1.astype(jnp.bfloat16), "row", scatter_dimension=0, tiled=True
        ).astype(jnp.float32),
        lax.psum_scatter(
            sum_shift1.astype(jnp.bfloat16), "row", scatter_dimension=0, tiled=True
        ).astype(jnp.float32),
        lax.psum_scatter(
            sum_biasq.astype(jnp.bfloat16), "row", scatter_dimension=0, tiled=True
        ).astype(jnp.float32),
        lax.psum_scatter(
            sum_biasv.astype(jnp.bfloat16), "row", scatter_dimension=0, tiled=True
        ).astype(jnp.float32),
        lax.psum_scatter(
            sum_biasp.astype(jnp.bfloat16), "row", scatter_dimension=0, tiled=True
        ).astype(jnp.float32),
        lax.psum_scatter(
            sum_gain2.astype(jnp.bfloat16), "row", scatter_dimension=0, tiled=True
        ).astype(jnp.float32),
        lax.psum_scatter(
            sum_shift2.astype(jnp.bfloat16), "row", scatter_dimension=0, tiled=True
        ).astype(jnp.float32),
        lax.psum_scatter(
            sum_bias1.astype(jnp.bfloat16), "row", scatter_dimension=0, tiled=True
        ).astype(jnp.float32),
        lax.psum_scatter(
            sum_bias2.astype(jnp.bfloat16), "row", scatter_dimension=0, tiled=True
        ).astype(jnp.float32),
    )
    return (
        result.astype(jnp.bfloat16),
        grad_inputs,
        out_qkv,
        out_proj,
        out_fc1,
        out_fc2,
        out_gain1,
        out_shift1,
        out_biasq,
        out_biasv,
        out_biasp,
        out_gain2,
        out_shift2,
        out_bias1,
        out_bias2,
    )


def solution(mesh):
    return jax.shard_map(
        per_device,
        mesh=mesh,
        in_specs=(
            P(("col", "row"), None),
            P("row", "col"),
            P("row", "col"),
            P("row", "col"),
            P("row", "col"),
            P(("col", "row")),
            P(("col", "row")),
            P(("col", "row")),
            P(("col", "row")),
            P(("col", "row")),
            P(("col", "row")),
            P(("col", "row")),
            P(("col", "row")),
            P(("col", "row")),
            P(("col", "row"), None),
        ),
        out_specs=(
            P(("col", "row"), None),
            P(("col", "row"), None),
            P("row", "col"),
            P("row", "col"),
            P("row", "col"),
            P("row", "col"),
            P(("col", "row")),
            P(("col", "row")),
            P(("col", "row")),
            P(("col", "row")),
            P(("col", "row")),
            P(("col", "row")),
            P(("col", "row")),
            P(("col", "row")),
            P(("col", "row")),
        ),
        check_vma=False,
    )
```

profile of v0, /device:TPU:0, one launch (start us, length us, event | category | flops | bytes accessed | tf_op | source)
XLA Modules:
  0.0 1211.3 jit_solution(12227109749676747950)
XLA Ops:
  48.5 59.8 %all-reduce.35 = (bf16[1024]{0:T(1024)(128)(2,1)S(1)}, bf16[1024]{0:T(1024)(128)(2,1)S(1)}, bf16[1024]{0:T(1024)(128)(2,1)S(1)}, bf16[1024]{0:T(1024)(128)(2,1)S...) all-reduce(bf16[1024]{0:T(1024)(128)(2,1)S(1)} %dynamic-update-slic, ...), channel_id=1, replica_groups=mesh['row'=2,'col'=16] {'col'}, use_global_device_ids=true, to_apply=%add.7 | all-reduce | flops 7168 | bytes 28672
  120.9 12.0 reshape.168
  144.3 55.4 %all_gather.108 = bf16[4096,64]{0,1:T(8,128)(2,1)} all-gather(bf16[2048,64]{0,1:T(8,128)(2,1)S(1)} %copy-done.11), channel_id=1, replica_groups=mesh['row'=2,'col'=16] {'row'}, dimensions={0}, use_global_device_ids=true | all-gather | bytes 786432 | tf_op jit(solution)/shard_map/all_gather | solution.py:126
  199.8 14.2 %copy.49 = bf16[2,784,3,1,512]{1,0,4,2,3:T(2,128)(2,1)} copy(bf16[2,784,3,1,512]{4,1,2,0,3:T(8,128)(2,1)} %bitcast.3) | data formatting | bytes 9633792 | tf_op jit(solution)/shard_map/all_to_all | solution.py:181
  214.0 11.7 squeeze.35
  225.7 32.2 %multiply_reduce_fusion.1 = (f32[8,1568]{1,0:T(8,128)S(1)}, f32[8,1568,1568]{1,2,0:T(8,128)}) fusion(bf16[1568,3,8,64]{0,3,2,1:T(8,128)(2,1)} %squeeze.35), kind=kOutput, calls=%fused_computation.6 | convolution fusion | flops 2556956416 | bytes 82134016 | tf_op jit(solution)/shard_map/while/body/eval_jaxpr/qhd,khd->hqk/dot_general | solution.py:53
  257.9 26.7 %fusion = f32[8,1568]{1,0:T(8,128)S(1)} fusion(f32[8,1568,1568]{1,2,0:T(8,128)} %get-tuple-element.94, f32[8,1568]{1,0:T(8,128)S(1)} %get-tuple-element.93), kind=kLoop, calls=%fused_computation.5 | loop fusion | flops 58994432 | bytes 78776320 | tf_op jit(solution)/shard_map/while/body/eval_jaxpr/reduce_sum | solution.py:58
  284.7 30.8 %fusion.38 = bf16[8,64,1568]{2,1,0:T(8,128)(2,1)S(1)} fusion(f32[8,1568,1568]{1,2,0:T(8,128)} %get-tuple-element.94, f32[8,1568]{1,0:T(8,128)S(1)} %fusion, f32[8,1568]{1,0:T(8,128)S(1)} %get-tuple-element.93, bf16[1568,3,8,64]{0,3,2,1:T(8,128)(2,1)} %squeeze.35), kind=kOutput, calls=%fused_computation.70 | convolution fusion | flops 2597109760 | bytes 86902784 | tf_op jit(solution)/shard_map/while/body/eval_jaxpr/hqk,khd->qhd/dot_general | solution.py:60
  325.2 14.5 %all-gather = bf16[2,1,128]{2,1,0:T(2,128)(2,1)S(1)} all-gather(bf16[1,1,128]{2,1,0:T(2,128)(2,1)S(1)} %bitcast.100), channel_id=1, replica_groups=mesh['row'=2,'col'=16] {'row'}, dimensions={0}, use_global_device_ids=true | all-gather | bytes 768 | tf_op jit(solution)/shard_map/all_gather | solution.py:134
  339.7 37.4 %all-gather.1 = bf16[16,1,256]{2,1,0:T(2,128)(2,1)S(1)} all-gather(bf16[1,1,256]{2,1,0:T(2,128)(2,1)S(1)} %bitcast.99), channel_id=1, replica_groups=mesh['row'=2,'col'=16] {'col'}, dimensions={0}, use_global_device_ids=true | all-gather | bytes 8704 | tf_op jit(solution)/shard_map/all_gather | solution.py:163
  390.7 39.0 %fusion.7 = (bf16[784,4096]{1,0:T(8,128)(2,1)}, f32[784,4096]{1,0:T(8,128)}) fusion(f32[4096]{0:T(1024)S(1)} %bitcast.97, bf16[1024,4096]{1,0:T(8,128)(2,1)} %all-gather.11.cloned.1.call-done, f32[784,1024]{1,0:T(8,128)} %copy-done.5, f32[1024]{0:T(1024)S(1)} %convert_element_type.201, f32[1024]{0:T(1024)S(1)} %convert_element_type.200, ...), kind=kOutput, calls=%fused_computation.14 | convolution fusion | flops 6792626176 | bytes 30898304 | tf_op jit(solution)/shard_map/dot_general | solution.py:197
  429.7 17.4 %fusion.53 = (bf16[4096]{0:T(1024)(128)(2,1)}, bf16[784,4096]{1,0:T(8,128)(2,1)}) fusion(f32[784,4096]{1,0:T(8,128)} %get-tuple-element.104, f32[4096]{0:T(1024)S(1)} %bitcast.98, bf16[4096,1024]{0,1:T(8,128)(2,1)} %all-gather.13.cloned.1.call-done, f32[784,1024]{1,0:T(8,128)S(1)} %copy-done.7), kind=kOutput, calls=%fused_computation.112 | convolution fusion | flops 6616002560 | bytes 30892032 | tf_op jit(solution)/shard_map/dot_general | solution.py:46
  467.0 20.3 %all-to-all-done.2 = bf16[784,2,512]{2,0,1:T(8,128)(2,1)S(1)} async-done(((bf16[784,2,512]{2,0,1:T(8,128)(2,1)}), bf16[784,2,512]{2,0,1:T(8,128)(2,1)S(1)}, u32[]{:S(2)}, u32[]{:S(2)}) %all-to-all-start.2) | async-done | bytes 1605664 | tf_op jit(solution)/shard_map/all_to_all | solution.py:232
  495.3 29.4 %fusion.35 = bf16[8,64,1568]{2,1,0:T(8,128)(2,1)} fusion(bf16[1568,8,64]{0,2,1:T(8,128)(2,1)S(1)} %squeeze.39, f32[8,1568,1568]{1,2,0:T(8,128)} %get-tuple-element.94, f32[8,1568]{1,0:T(8,128)S(1)} %log_add_fusion), kind=kOutput, calls=%fused_computation.69 | convolution fusion | flops 2577440768 | bytes 81937408 | tf_op jit(solution)/shard_map/while/body/eval_jaxpr/hqk,qhd->khd/dot_general | solution.py:74
  524.7 56.6 %multiply_reduce_fusion = (f32[8,1568]{1,0:T(8,128)S(1)}, f32[8,1568,1568]{1,2,0:T(8,128)}) fusion(f32[8,1568,1568]{1,2,0:T(8,128)} %get-tuple-element.94, f32[8,1568]{1,0:T(8,128)S(1)} %log_add_fusion, bf16[1568,8,64]{0,2,1:T(8,128)(2,1)S(1)} %squeeze.39, bf16[1568,3,8,64]{0,3,2,1:T(8,128)(2,1)} %squeeze.35), kind=kOutput, calls=%fused_computation.1 | convolution fusion | flops 2596294400 | bytes 165578752 | tf_op jit(solution)/shard_map/while/body/eval_jaxpr/qhd,khd->hqk/dot_general | solution.py:77
  581.3 64.8 %multiply_convert_fusion = bf16[8,1568,1568]{1,2,0:T(8,128)(2,1)} fusion(f32[8,1568,1568]{1,2,0:T(8,128)} %get-tuple-element.99, f32[8,1568,1568]{1,2,0:T(8,128)} %get-tuple-element.94, f32[8,1568]{1,0:T(8,128)S(1)} %get-tuple-element.98, f32[8,1568]{1,0:T(8,128)S(1)} %log_add_fusion), kind=kLoop, calls=%fused_computation | loop fusion | flops 98344960 | bytes 196790272 | tf_op jit(solution)/shard_map/while/body/eval_jaxpr/convert_element_type | solution.py:81
  646.1 20.4 %multiply_convert_fusion.1 = bf16[8,64,1568]{2,1,0:T(8,128)(2,1)} fusion(bf16[8,1568,1568]{1,2,0:T(8,128)(2,1)} %multiply_convert_fusion, bf16[1568,3,8,64]{0,3,2,1:T(8,128)(2,1)} %squeeze.35), kind=kOutput, calls=%fused_computation.50 | convolution fusion | flops 2519236608 | bytes 45056000 | tf_op jit(solution)/shard_map/while/body/eval_jaxpr/hqk,qhd->khd/dot_general | solution.py:85
  666.5 21.0 %multiply_convert_fusion.2 = bf16[8,64,1568]{2,1,0:T(8,128)(2,1)} fusion(bf16[8,1568,1568]{1,2,0:T(8,128)(2,1)} %multiply_convert_fusion, bf16[1568,3,8,64]{0,3,2,1:T(8,128)(2,1)} %squeeze.35), kind=kOutput, calls=%fused_computation.51 | convolution fusion | flops 2519236608 | bytes 45056000 | tf_op jit(solution)/shard_map/while/body/eval_jaxpr/hqk,khd->qhd/dot_general | solution.py:82
  714.1 13.9 %pad_maximum_fusion = bf16[1568,3,1,512]{3,1,2,0:T(4,128)(2,1)} fusion(bf16[1568,1,1,512]{3,1,2,0:T(2,128)(2,1)S(1)} %copy.60, bf16[1568,1,1,512]{3,1,2,0:T(2,128)(2,1)} %copy.59, bf16[1568,1,1,512]{3,1,2,0:T(2,128)(2,1)} %copy.58), kind=kLoop, calls=%fused_computation.39 | loop fusion | flops 14450688 | bytes 9633792 | tf_op jit(solution)/shard_map/while/body/eval_jaxpr/stack | solution.py:88
  740.3 65.6 %all-to-all-done.3 = bf16[1568,3,1,512]{3,1,2,0:T(4,128)(2,1)} async-done(((bf16[1568,3,1,512]{3,1,2,0:T(4,128)(2,1)}), bf16[1568,3,1,512]{3,1,2,0:T(4,128)(2,1)}, u32[]{:S(2)}, u32[]{:S(2)}) %all-to-all-start.3) | async-done | bytes 4816928 | tf_op jit(solution)/shard_map/all_to_all | solution.py:241
  821.6 12.1 reshape.172
  833.8 11.4 convolution_convert_fusion.2
  845.9 15.0 %convolution_convert_fusion.1 = bf16[1024,4096]{1,0:T(8,128)(2,1)} fusion(bf16[784,4096]{1,0:T(8,128)(2,1)} %get-tuple-element.102, f32[784,1024]{1,0:T(8,128)} %copy-done.5, f32[1024]{0:T(1024)S(1)} %copy-done.32, f32[1024]{0:T(1024)S(1)} %copy-done.23, f32[784]{0:T(1024)S(1)} %copy-done.25, f32[784]{0:T(1024)S(1)} %copy-done.17), kind=kOutput, calls=%fused_computation.38 | convolution fusion | flops 6584877056 | bytes 18036864 | tf_op jit(solution)/shard_map/dot_general | solution.py:40
  860.9 14.9 %convolution_convert_fusion = bf16[4096,1024]{0,1:T(8,128)(2,1)} fusion(bf16[784,4096]{1,0:T(8,128)(2,1)} %get-tuple-element.103, f32[784,1024]{1,0:T(8,128)} %param.29), kind=kOutput, calls=%fused_computation.37 | convolution fusion | flops 6581665792 | bytes 18022400 | tf_op jit(solution)/shard_map/dot_general | solution.py:40
  879.4 47.0 %reduce-scatter.9.cloned.1.call-done = bf16[1024,192]{0,1:T(8,128)(2,1)} async-done(((bf16[1024,3072]{0,1:T(8,128)(2,1)}), bf16[1024,192]{0,1:T(8,128)(2,1)}) %reduce-scatter.9.cloned.1.call-update) | async-done | bytes 393232 | tf_op jit(solution)/shard_map/reduce_scatter | solution.py:271
  941.9 61.2 %all-reduce.34 = (bf16[1024]{0:T(1024)(128)(2,1)S(1)}, bf16[1024]{0:T(1024)(128)(2,1)S(1)}, bf16[1024]{0:T(1024)(128)(2,1)S(1)}, bf16[1024]{0:T(1024)(128)(2,1)S...) all-reduce(bf16[1024]{0:T(1024)(128)(2,1)S(1)} %dynamic-update-slic, ...), channel_id=1, replica_groups=mesh['row'=2,'col'=16] {'col'}, use_global_device_ids=true, to_apply=%add.15 | all-reduce | flops 13312 | bytes 53248
  1003.1 30.9 %reduce-scatter.17.cloned.1.call-done = bf16[1024,256]{1,0:T(8,128)(2,1)} async-done(((bf16[1024,4096]{1,0:T(8,128)(2,1)}), bf16[1024,256]{1,0:T(8,128)(2,1)}) %reduce-scatter.17.cloned.1.call-update) | async-done | bytes 524304 | tf_op jit(solution)/shard_map/reduce_scatter | solution.py:277
  1034.1 12.5 %add_convert_fusion.1 = bf16[784,1024]{1,0:T(8,128)(2,1)} fusion(f32[784,1024]{1,0:T(8,128)} %copy-done.5, f32[1024]{0:T(1024)S(1)} %convert_element_type.205, bf16[784,4096]{1,0:T(8,128)(2,1)} %get-tuple-element.103, bf16[4096,1024]{0,1:T(8,128)(2,1)} %all-gather.13.cloned.1.call-done), kind=kOutput, calls=%fused_computation.65 | convolution fusion | flops 6579077120 | bytes 19632128 | tf_op jit(solution)/shard_map/dot_general | solution.py:202
  1056.9 84.3 %reduce-scatter.21.cloned.1.call-done = bf16[4096,64]{0,1:T(8,128)(2,1)} async-done(((bf16[4096,1024]{0,1:T(8,128)(2,1)}), bf16[4096,64]{0,1:T(8,128)(2,1)}) %reduce-scatter.21.cloned.1.call-update) | async-done | bytes 524304 | tf_op jit(solution)/shard_map/reduce_scatter | solution.py:280
  1155.0 13.8 %reduce-scatter.11.cloned.1.call-done = bf16[512,192]{0,1:T(8,128)(2,1)} async-done(((bf16[1024,192]{0,1:T(8,128)(2,1)}), bf16[512,192]{0,1:T(8,128)(2,1)}) %reduce-scatter.11.cloned.1.call-update) | async-done | bytes 196624 | tf_op jit(solution)/shard_map/reduce_scatter | solution.py:326
  1170.5 15.2 %reduce-scatter.19.cloned.1.call-done = bf16[512,256]{1,0:T(8,128)(2,1)} async-done(((bf16[1024,256]{1,0:T(8,128)(2,1)}), bf16[512,256]{1,0:T(8,128)(2,1)}) %reduce-scatter.19.cloned.1.call-update) | async-done | bytes 262160 | tf_op jit(solution)/shard_map/reduce_scatter | solution.py:332
  1187.5 15.0 %reduce-scatter.23.cloned.1.call-done = bf16[2048,64]{0,1:T(8,128)(2,1)} async-done(((bf16[4096,64]{0,1:T(8,128)(2,1)}), bf16[2048,64]{0,1:T(8,128)(2,1)}) %reduce-scatter.23.cloned.1.call-update) | async-done | bytes 262160 | tf_op jit(solution)/shard_map/reduce_scatter | solution.py:335
  (230 shorter events, 215.8 us)
Async XLA Ops:
  7.2 102.9 %copy-start = (bf16[784,1024]{1,0:T(8,128)(2,1)S(1)}, bf16[784,1024]{1,0:T(8,128)(2,1)}, u32[]{:S(2)}) copy-start(bf16[784,1024]{1,0:T(8,128)(2,1)} %param.15) | copy-start | bytes 4816900
  7.2 103.6 %all-gather.7.cloned.1.call-start = ((), (), s32[]{:S(2)}) async-start(), calls=%async_computation.12 | async-start | bytes 6684672 | tf_op jit(solution)/shard_map/all_gather | solution.py:152
  17.9 366.4 %all-gather.9.cloned.1.call-start = ((), (), s32[]{:S(2)}) async-start(), calls=%async_computation.13 | async-start | bytes 2228224 | tf_op jit(solution)/shard_map/all_gather | solution.py:153
  23.2 367.5 %all-gather.11.cloned.1.call-start = ((), (), s32[]{:S(2)}) async-start(), calls=%async_computation.14 | async-start | bytes 8912896 | tf_op jit(solution)/shard_map/all_gather | solution.py:154
  108.3 12.6 %copy-start.18 = (f32[1024]{0:T(1024)}, f32[1024]{0:T(1024)S(1)}, u32[]{:S(2)}) copy-start(f32[1024]{0:T(1024)S(1)} %convert_element_type.190) | copy-start | bytes 12292
  108.3 12.6 %copy-start.29 = (f32[1024]{0:T(1024)}, f32[1024]{0:T(1024)S(1)}, u32[]{:S(2)}) copy-start(f32[1024]{0:T(1024)S(1)} %convert_element_type.191) | copy-start | bytes 12292
  138.3 61.5 %all-to-all-start = ((bf16[784,3,2,512]{3,0,1,2:T(8,128)(2,1)}), bf16[784,3,2,512]{3,0,1,2:T(8,128)(2,1)}, u32[]{:S(2)}, u32[]{:S(2)}) async-start(bf16[784,3,2,512]{3,0,1,2:T(8,128)(2,1)} %copy.48), calls=%async_computation | async-start | bytes 9633792 | tf_op jit(solution)/shard_map/all_to_all | solution.py:181
  144.3 285.4 %all-gather.13.cloned.1.call-start = ((), (), s32[]{:S(2)}) async-start(), calls=%async_computation.15 | async-start | bytes 8912896 | tf_op jit(solution)/shard_map/all_gather | solution.py:155
  257.9 26.7 %copy-start.9 = (f32[8,1568]{1,0:T(8,128)}, f32[8,1568]{1,0:T(8,128)S(1)}, u32[]{:S(2)}) copy-start(f32[8,1568]{1,0:T(8,128)S(1)} %get-tuple-element.93) | copy-start | bytes 150532
  284.7 30.8 %copy-start.12 = (f32[8,1568]{1,0:T(8,128)}, f32[8,1568]{1,0:T(8,128)S(1)}, u32[]{:S(2)}) copy-start(f32[8,1568]{1,0:T(8,128)S(1)} %fusion) | copy-start | bytes 150532
  321.5 55.7 %all-to-all-start.1 = ((bf16[2,2,200704]{2,1,0:T(2,128)(2,1)}), bf16[2,2,200704]{2,1,0:T(2,128)(2,1)S(1)}, u32[]{:S(2)}, u32[]{:S(2)}) async-start(bf16[2,2,200704]{2,1,0:T(2,128)(2,1)} %reshape.277), calls=%async_computation.1 | async-start | bytes 3211264 | tf_op jit(solution)/shard_map/all_to_all | solution.py:186
  325.2 132.9 %copy-start.22 = (f32[1024]{0:T(1024)}, f32[1024]{0:T(1024)S(1)}, u32[]{:S(2)}) copy-start(f32[1024]{0:T(1024)S(1)} %convert_element_type.200) | copy-start | bytes 12292
  325.2 65.5 %copy-start.31 = (f32[1024]{0:T(1024)}, f32[1024]{0:T(1024)S(1)}, u32[]{:S(2)}) copy-start(f32[1024]{0:T(1024)S(1)} %convert_element_type.201) | copy-start | bytes 12292
  388.5 69.6 %copy-start.16 = (f32[784]{0:T(1024)}, f32[784]{0:T(1024)S(1)}, u32[]{:S(2)}) copy-start(f32[784]{0:T(1024)S(1)} %broadcast_multiply_fusion.4) | copy-start | bytes 9412
  390.6 67.5 %copy-start.24 = (f32[784]{0:T(1024)}, f32[784]{0:T(1024)S(1)}, u32[]{:S(2)}) copy-start(f32[784]{0:T(1024)S(1)} %add_rsqrt_fusion) | copy-start | bytes 9412
  390.7 39.0 %copy-start.7 = (f32[784,1024]{1,0:T(8,128)S(1)}, f32[784,1024]{1,0:T(8,128)}, u32[]{:S(2)}) copy-start(f32[784,1024]{1,0:T(8,128)} %param.29) | copy-start | bytes 9633796
  429.7 17.4 %copy-start.6 = (f32[784,1024]{1,0:T(8,128)S(1)}, f32[784,1024]{1,0:T(8,128)}, u32[]{:S(2)}) copy-start(f32[784,1024]{1,0:T(8,128)} %copy-done.5) | copy-start | bytes 9633796
  429.7 17.4 %copy-start.38 = (bf16[1024,4096]{1,0:T(8,128)(2,1)S(1)}, bf16[1024,4096]{1,0:T(8,128)(2,1)}, u32[]{:S(2)}) copy-start(bf16[1024,4096]{1,0:T(8,128)(2,1)} %all-gather.11.cloned.1.call-done) | copy-start | bytes 25165828
  463.3 24.0 %all-to-all-start.2 = ((bf16[784,2,512]{2,0,1:T(8,128)(2,1)}), bf16[784,2,512]{2,0,1:T(8,128)(2,1)S(1)}, u32[]{:S(2)}, u32[]{:S(2)}) async-start(bf16[784,2,512]{2,0,1:T(8,128)(2,1)} %bitcast.85), calls=%async_computation.2 | async-start | bytes 3211264 | tf_op jit(solution)/shard_map/all_to_all | solution.py:232
  728.0 77.9 %all-to-all-start.3 = ((bf16[1568,3,1,512]{3,1,2,0:T(4,128)(2,1)}), bf16[1568,3,1,512]{3,1,2,0:T(4,128)(2,1)}, u32[]{:S(2)}, u32[]{:S(2)}) async-start(bf16[1568,3,1,512]{3,1,2,0:T(4,128)(2,1)} %pad_maximum_fusion), calls=%async_computation.3 | async-start | bytes 12845056 | tf_op jit(solution)/shard_map/all_to_all | solution.py:241
  734.7 141.2 %reduce-scatter.13.cloned.1.call-start = ((), (), s32[]{:S(2)}) async-start(), calls=%async_computation.18 | async-start | bytes 2228224 | tf_op jit(solution)/shard_map/reduce_scatter | solution.py:274
  739.9 186.6 %reduce-scatter.9.cloned.1.call-start = ((), (), s32[]{:S(2)}) async-start(), calls=%async_computation.16 | async-start | bytes 6684672 | tf_op jit(solution)/shard_map/reduce_scatter | solution.py:271
  821.6 12.1 %copy-start.15 = (f32[784]{0:T(1024)S(1)}, f32[784]{0:T(1024)}, u32[]{:S(2)}) copy-start(f32[784]{0:T(1024)} %copy-done.14) | copy-start | bytes 9412
  821.6 12.1 %copy-start.19 = (f32[1024]{0:T(1024)S(1)}, f32[1024]{0:T(1024)}, u32[]{:S(2)}) copy-start(f32[1024]{0:T(1024)} %copy-done.18) | copy-start | bytes 12292
  821.6 12.1 %copy-start.21 = (f32[784]{0:T(1024)S(1)}, f32[784]{0:T(1024)}, u32[]{:S(2)}) copy-start(f32[784]{0:T(1024)} %copy-done.20) | copy-start | bytes 9412
  821.6 12.1 %copy-start.30 = (f32[1024]{0:T(1024)S(1)}, f32[1024]{0:T(1024)}, u32[]{:S(2)}) copy-start(f32[1024]{0:T(1024)} %copy-done.29) | copy-start | bytes 12292
  845.2 188.8 %reduce-scatter.17.cloned.1.call-start = ((), (), s32[]{:S(2)}) async-start(), calls=%async_computation.20 | async-start | bytes 8912896 | tf_op jit(solution)/shard_map/reduce_scatter | solution.py:277
  860.8 280.4 %reduce-scatter.21.cloned.1.call-start = ((), (), s32[]{:S(2)}) async-start(), calls=%async_computation.22 | async-start | bytes 8912896 | tf_op jit(solution)/shard_map/reduce_scatter | solution.py:280
  875.8 277.6 %reduce-scatter.15.cloned.1.call-start = ((), (), s32[]{:S(2)}) async-start(), calls=%async_computation.19 | async-start | bytes 196608 | tf_op jit(solution)/shard_map/reduce_scatter | solution.py:329
  876.6 292.2 %reduce-scatter.11.cloned.1.call-start = ((), (), s32[]{:S(2)}) async-start(), calls=%async_computation.17 | async-start | bytes 589824 | tf_op jit(solution)/shard_map/reduce_scatter | solution.py:326
  926.5 259.2 %reduce-scatter.19.cloned.1.call-start = ((), (), s32[]{:S(2)}) async-start(), calls=%async_computation.21 | async-start | bytes 786432 | tf_op jit(solution)/shard_map/reduce_scatter | solution.py:332
  1034.0 168.4 %reduce-scatter.23.cloned.1.call-start = ((), (), s32[]{:S(2)}) async-start(), calls=%async_computation.23 | async-start | bytes 786432 | tf_op jit(solution)/shard_map/reduce_scatter | solution.py:335
  (26 other events, 108.6 us)
Sparse Core Ops, SparseCore 0:
  18.0 62.1 all-gather.6
  82.3 40.4 all-gather.8
  125.0 76.2 all-gather.10
  203.3 72.4 all-gather.12
  740.0 59.4 reduce-scatter.12
  845.3 81.1 reduce-scatter.8
  930.6 103.4 reduce-scatter.16
  1038.1 103.0 reduce-scatter.20
  1143.4 9.9 reduce-scatter.14
  1155.5 13.1 reduce-scatter.10
  1171.0 14.6 reduce-scatter.18
  1187.8 14.6 reduce-scatter.22
where the time goes:
time: 1220 us; the launch traced here: 1210 us
  matrix products  343 us (28%)
  waiting for transfers between devices  300 us (25%)
  blocking collectives  264 us (22%)
  other arithmetic  133 us (11%)
  local copies, waits for them, and re-layouts  131 us (11%)
  starting transfers between devices  20.9 us (2%)
  between operations  19.1 us (2%)
    unnamed x4, blocking collectives  131 us
    reduce_scatter x1, waiting for transfers between devices, per_device(): lax.psum_scatter(grad_fc2.astype(jnp.bfloat16), 'col', scatter_dimension=...  84.3 us
    all_to_all x1, waiting for transfers between devices, per_device(): lax.all_to_all(grad_triple.reshape(col_rows, 3, 1, per_group), 'row', spl...  65.6 us
    convert_element_type x1, other arithmetic, clip_backward(): (weights_full * (grad_weights - row_delta)).astype(jnp.bfloat16)  64.8 us
    dot_general x1, matrix products, clip_backward(): jnp.einsum('qhd,khd->hqk', grad_mixed, value_rows, preferred_element_type...  56.6 us
    all_gather x1, blocking collectives, per_device(): lax.all_gather(w_fc2, 'row', axis=0, tiled=True)  55.4 us
    reduce_scatter x1, waiting for transfers between devices, per_device(): lax.psum_scatter(grad_qkv.astype(jnp.bfloat16), 'col', scatter_dimension=...  47 us
    dot_general x4, matrix products, inner_rows(): lax.dot_general(first, second, (((0,), (0,)), ((), ())), preferred_elemen...  46.3 us
  transfers between devices with their start and end apart: 16, of which 9 were waited for; matrix products, arithmetic and copies ran while one was open for 27% of the time, Pallas kernels for 0%

commit v1 on v0

--- a/solution.py
+++ b/solution.py
@@ -3,6 +3,8 @@
 import jax
 import jax.numpy as jnp
 from jax import lax
+from jax.experimental import pallas as pl
+from jax.experimental.pallas import tpu as pltpu
 from jax.sharding import PartitionSpec as P
 
 D = 1024
@@ -382,9 +384,738 @@
     )
 
 
+bf16 = jnp.bfloat16
+f32 = jnp.float32
+FF = 4096
+ROWS_QKV, ROWS_A = 768, 784
+ROWS_FC, ROWS_PROJ, ROWS_B = 1024, 256, 2304
+VMEM_LIMIT = 62 * 1024 * 1024
+NT = (((1,), (1,)), ((), ()))
+TN = (((0,), (0,)), ((), ()))
+
+
+def params(limit=VMEM_LIMIT):
+    return pltpu.CompilerParams(vmem_limit_bytes=limit)
+
+
+def cost(flops, data, trans=0):
+    return pl.CostEstimate(flops=int(flops), bytes_accessed=int(data), transcendentals=int(trans))
+
+
+def once(shape, index):
+    return pl.BlockSpec(shape, index, pipeline_mode=pl.Buffered(1))
+
+
+def halves_cat(first, second):
+    return jnp.concatenate([first[:, :64], second[:, :64]], axis=1)
+
+
+def row_stats(value):
+    average = jnp.mean(value, axis=-1, keepdims=True)
+    centred = value - average
+    spread = jnp.mean(centred * centred, axis=-1, keepdims=True)
+    inverse = lax.rsqrt(spread + EPSILON)
+    return centred * inverse, inverse
+
+
+def pack_qkv(block):
+    tail = block[:, 128:]
+    return jnp.concatenate(
+        [block[:, :128], jnp.concatenate([tail[:256], tail[256:]], axis=1)], axis=0
+    )
+
+
+def unpack_qkv(rows):
+    tail = rows[512:768]
+    return jnp.concatenate(
+        [rows[:512], jnp.concatenate([tail[:, :64], tail[:, 64:]], axis=0)], axis=1
+    )
+
+
+def pack_proj(block):
+    return jnp.concatenate([block[:256], block[256:]], axis=1)
+
+
+def unpack_proj(rows):
+    return jnp.concatenate([rows[:, :64], rows[:, 64:]], axis=0)
+
+
+def pack_fc1(block):
+    return jnp.concatenate([block[:, :128], block[:, 128:]], axis=0)
+
+
+def unpack_fc1(rows):
+    return jnp.concatenate([rows[:512], rows[512:]], axis=1)
+
+
+def pack_fc2(block):
+    return block.reshape(4, 2, 256, 64).transpose(0, 2, 1, 3).reshape(1024, 128)
+
+
+def unpack_fc2(rows):
+    return rows.reshape(4, 256, 2, 64).transpose(0, 2, 1, 3).reshape(2048, 64)
+
+
+def assemble_qkv(w_refs, w_out):
+    for r in range(2):
+        w0, w1 = w_refs[r][0][0], w_refs[r][1][0]
+        a0, b0 = w0[:512], w0[512:768]
+        a1, b1 = w1[:512], w1[512:768]
+        lo = slice(512 * r, 512 * r + 256)
+        hi = slice(512 * r + 256, 512 * r + 512)
+        w_out[512 * r : 512 * r + 512, 0:128] = a0
+        w_out[lo, 128:256] = jnp.concatenate([b0[:, :64], a1[:256, :64]], axis=1)
+        w_out[hi, 128:256] = jnp.concatenate([b0[:, 64:], a1[256:, :64]], axis=1)
+        w_out[lo, 256:384] = jnp.concatenate([a1[:256, 64:], b1[:, :64]], axis=1)
+        w_out[hi, 256:384] = jnp.concatenate([a1[256:, 64:], b1[:, 64:]], axis=1)
+
+
+def qkv_body(tok, x_own, x_oth, w00, w01, w10, w11, gain, shift, bias, h_ref, qkv_ref, w_sc):
+    step = pl.program_id(0)
+
+    @pl.when(step == 0)
+    def _():
+        for half, x_ref in enumerate((x_own, x_oth)):
+            for i in range(tok // 112):
+                rows = x_ref[i * 112 : (i + 1) * 112, :].astype(f32)
+                normed, _ = row_stats(rows)
+                h_ref[half * tok + i * 112 : half * tok + (i + 1) * 112, :] = (
+                    normed * gain[...] + shift[...]
+                ).astype(bf16)
+
+    assemble_qkv(((w00, w01), (w10, w11)), w_sc)
+
+    def project(rows):
+        out = jnp.dot(h_ref[0:rows, :], w_sc[...], preferred_element_type=f32) + bias[...]
+        out = out.astype(bf16)
+        for i in range(3):
+            tile = 3 * step + i
+            part, column = tile // 8, tile % 8
+            qkv_ref[part, 0:rows, pl.ds(pl.multiple_of(column * 128, 128), 128)] = out[
+                :, i * 128 : (i + 1) * 128
+            ]
+
+    @pl.when(step < 2)
+    def _():
+        project(tok)
+
+    @pl.when(step >= 2)
+    def _():
+        project(2 * tok)
+
+
+def qkv_call(x_own, x_oth, table, gathered, gain, shift, bias):
+    tok = x_own.shape[0]
+
+    def weight(r, k):
+        return pl.BlockSpec((1, ROWS_A, 128), lambda j, t: (t[r * 16 + 2 * j + k], 0, 0))
+
+    return pl.pallas_call(
+        lambda t, *refs: qkv_body(tok, *refs),
+        out_shape=(
+            jax.ShapeDtypeStruct((2 * tok, D), bf16),
+            jax.ShapeDtypeStruct((3, 2 * tok, D), bf16),
+        ),
+        grid_spec=pltpu.PrefetchScalarGridSpec(
+            num_scalar_prefetch=1,
+            grid=(8,),
+            in_specs=[
+                once((tok, D), lambda j, t: (0, 0)),
+                once((tok, D), lambda j, t: (0, 0)),
+                weight(0, 0),
+                weight(0, 1),
+                weight(1, 0),
+                weight(1, 1),
+                once((1, D), lambda j, t: (0, 0)),
+                once((1, D), lambda j, t: (0, 0)),
+                pl.BlockSpec((1, 384), lambda j, t: (0, j)),
+            ],
+            out_specs=[
+                once((2 * tok, D), lambda j, t: (0, 0)),
+                once((3, 2 * tok, D), lambda j, t: (0, 0, 0)),
+            ],
+            scratch_shapes=[pltpu.VMEM((D, 384), bf16)],
+        ),
+        compiler_params=params(),
+        cost_estimate=cost(2 * tok * D * D * 5, 24e6),
+        name="qkv_forward",
+    )(table, x_own, x_oth, gathered, gathered, gathered, gathered, gain, shift, bias)
+
+
+def attend_body(tok, keys, chunk, q_ref, k_ref, v_ref, o_ref, l_ref, *scratch):
+    vt_a, vt_b, qm, s_a, s_b, m_a, m_b, acc_sc, o_sc = scratch
+    count = keys // chunk
+    lane = lax.broadcasted_iota(jnp.int32, (1, 128), 1)
+    q2 = q_ref[...] * jnp.asarray(HD**-0.5, bf16)
+    zero = jnp.zeros_like(q2)
+
+    def stage(q_head, s_w, m_w, s_r, m_r, vt_r):
+        peak = jnp.max(m_r[...], axis=0, keepdims=True)
+        acc_sc[...] = jnp.zeros_like(acc_sc)
+        qm[...] = q_head
+        m_w[...] = jnp.full_like(m_w, -jnp.inf)
+        for i in range(count):
+            rows = slice(i * chunk, (i + 1) * chunk)
+            s = lax.dot_general(k_ref[rows, :], qm[...], NT, preferred_element_type=f32)
+            s_w[rows, :] = s
+            m_w[...] = jnp.maximum(m_w[...], jnp.max(s.reshape(chunk // 8, 8, tok), axis=0))
+            p = jnp.exp(s_r[rows, :] - peak).astype(bf16)
+            acc_sc[...] += jnp.dot(vt_r[i], p, preferred_element_type=f32)
+        acc = acc_sc[...]
+        total = acc[64:65]
+        return acc[0:64] * (1.0 / total), peak + jnp.log(total)
+
+    out_b, lse_b = stage(jnp.where(lane < 64, q2, zero), s_a, m_a, s_b, m_b, vt_b)
+    o_ref[0:64] = o_sc[0:64].astype(bf16)
+    o_ref[64:128] = out_b.astype(bf16)
+    l_ref[0] = o_sc[64:65]
+    l_ref[1] = lse_b
+    ones = jnp.ones((16, chunk), bf16)
+    for i in range(count):
+        vt = v_ref[i * chunk : (i + 1) * chunk, :].T
+        vt_a[i, 0:64] = vt[0:64]
+        vt_a[i, 64:80] = ones
+        vt_b[i, 0:64] = vt[64:128]
+        vt_b[i, 64:80] = ones
+    out_a, lse_a = stage(jnp.where(lane < 64, zero, q2), s_b, m_b, s_a, m_a, vt_a)
+    o_sc[0:64] = out_a
+    o_sc[64:65] = lse_a
+
+
+def attend_call(qkv, tok, chunk=224):
+    keys = qkv.shape[1]
+    pairs = H // 2
+
+    def column(part, rows):
+        return pl.BlockSpec((None, rows, 128), lambda g: (part, 0, jnp.minimum(g, pairs - 1)))
+
+    def behind(g):
+        return jnp.maximum(g - 1, 0)
+
+    return pl.pallas_call(
+        lambda *refs: attend_body(tok, keys, chunk, *refs),
+        out_shape=(
+            jax.ShapeDtypeStruct((D, tok), bf16),
+            jax.ShapeDtypeStruct((H, 1, tok), f32),
+        ),
+        grid=(pairs + 1,),
+        in_specs=[column(0, tok), column(1, keys), column(2, keys)],
+        out_specs=[
+            pl.BlockSpec((128, tok), lambda g: (behind(g), 0)),
+            pl.BlockSpec((2, 1, tok), lambda g: (behind(g), 0, 0)),
+        ],
+        scratch_shapes=[
+            pltpu.VMEM((keys // chunk, 80, chunk), bf16),
+            pltpu.VMEM((keys // chunk, 80, chunk), bf16),
+            pltpu.VMEM((tok, 128), bf16),
+            pltpu.VMEM((keys, tok), f32),
+            pltpu.VMEM((keys, tok), f32),
+            pltpu.VMEM((8, tok), f32),
+            pltpu.VMEM((8, tok), f32),
+            pltpu.VMEM((80, tok), f32),
+            pltpu.VMEM((72, tok), f32),
+        ],
+        compiler_params=params(),
+        cost_estimate=cost(16 * 4 * tok * keys * 256, 12e6, 16 * tok * keys),
+        name="attention_forward",
+    )(qkv, qkv, qkv)
+
+
+def attend_back_body(tok, keys, chunk, q_ref, k_ref, v_ref, g_ref, o_ref, l_ref, out_ref, *scratch):
+    qx, gx, q_t, g_t, dq_sc = scratch
+    lane = lax.broadcasted_iota(jnp.int32, (1, 128), 1)
+    row = lax.broadcasted_iota(jnp.int32, (128, 1), 0)
+    q2 = q_ref[...] * jnp.asarray(HD**-0.5, bf16)
+    grad = g_ref[...]
+    qx[:, 0:128] = q2
+    gx[:, 0:128] = grad
+    q_t[...] = q2.T
+    g_t[...] = grad.T
+    prod = g_t[...].astype(f32) * o_ref[...].astype(f32)
+
+    def split(value):
+        terms, rest = [], value
+        for _ in range(3):
+            term = rest.astype(bf16).astype(f32)
+            terms.append(term)
+            rest = rest - term
+        return terms
+
+    s_col = jnp.zeros((128, tok), f32)
+    d_col = jnp.zeros((128, tok), f32)
+    for h in range(2):
+        delta = jnp.sum(prod[h * 64 : h * 64 + 64], axis=0, keepdims=True)
+        for t, (a, b) in enumerate(zip(split(-l_ref[h]), split(-delta))):
+            s_col = jnp.where(row == h * 4 + t, a, s_col)
+            d_col = jnp.where(row == h * 4 + t, b, d_col)
+    qx[:, 128:256] = s_col.astype(bf16).T
+    gx[:, 128:256] = d_col.astype(bf16).T
+    dq_sc[...] = jnp.zeros_like(dq_sc)
+    for i in range(keys // chunk):
+        rows = slice(i * chunk, (i + 1) * chunk)
+        ks, vs = k_ref[rows, :], v_ref[rows, :]
+        dvs, dks, dq = [], [], None
+        for h in range(2):
+            mine = (lane >= h * 64) & (lane < h * 64 + 64)
+            pick = jnp.broadcast_to(
+                ((lane >= h * 4) & (lane < h * 4 + 3)).astype(bf16), (chunk, 128)
+            )
+            km = jnp.where(mine, ks, jnp.zeros_like(ks))
+            vm = jnp.where(mine, vs, jnp.zeros_like(vs))
+            p = jnp.exp(
+                lax.dot_general(
+                    qx[...], jnp.concatenate([km, pick], 1), NT, preferred_element_type=f32
+                )
+            )
+            dp = lax.dot_general(
+                gx[...], jnp.concatenate([vm, pick], 1), NT, preferred_element_type=f32
+            )
+            ds = (p * dp).astype(bf16)
+            p_low = p.astype(bf16)
+            head = slice(h * 64, h * 64 + 64)
+            dvs.append(jnp.dot(g_t[head], p_low, preferred_element_type=f32))
+            dks.append(jnp.dot(q_t[head], ds, preferred_element_type=f32))
+            part = jnp.dot(ds, km, preferred_element_type=f32)
+            dq = part if dq is None else dq + part
+        dq_sc[...] += dq
+        out_ref[1, rows, :] = jnp.concatenate(dks, 0).T.astype(bf16)
+        out_ref[2, rows, :] = jnp.concatenate(dvs, 0).T.astype(bf16)
+    out_ref[0, 0:tok, :] = (dq_sc[...] * HD**-0.5).astype(bf16)
+    out_ref[0, tok:keys, :] = jnp.zeros((keys - tok, 128), bf16)
+
+
+def attend_back_call(qkv, grad, mixed, logsum, chunk=224):
+    tok = grad.shape[0]
+    keys = qkv.shape[1]
+
+    def column(part, rows):
+        return pl.BlockSpec((None, rows, 128), lambda g: (part, 0, g))
+
+    return pl.pallas_call(
+        lambda *refs: attend_back_body(tok, keys, chunk, *refs),
+        out_shape=jax.ShapeDtypeStruct((3, keys, D), bf16),
+        grid=(H // 2,),
+        in_specs=[
+            column(0, tok),
+            column(1, keys),
+            column(2, keys),
+            pl.BlockSpec((tok, 128), lambda g: (0, g)),
+            pl.BlockSpec((128, tok), lambda g: (g, 0)),
+            pl.BlockSpec((2, 1, tok), lambda g: (g, 0, 0)),
+        ],
+        out_specs=pl.BlockSpec((3, keys, 128), lambda g: (0, 0, g)),
+        scratch_shapes=[
+            pltpu.VMEM((tok, 256), bf16),
+            pltpu.VMEM((tok, 256), bf16),
+            pltpu.VMEM((128, tok), bf16),
+            pltpu.VMEM((128, tok), bf16),
+            pltpu.VMEM((tok, 128), f32),
+        ],
+        compiler_params=params(),
+        cost_estimate=cost(16 * 8 * tok * keys * 256, 24e6, 16 * tok * keys),
+        name="attention_backward",
+    )(qkv, qkv, qkv, grad, mixed, logsum)
+
+
+def gelu_parts(value):
+    size = jnp.abs(value)
+    bell = jnp.exp(-0.5 * value * value)
+    t = 1.0 / (1.0 + (0.3275911 * 2.0**-0.5) * size)
+    poly = t * (
+        0.254829592
+        + t * (-0.284496736 + t * (1.421413741 + t * (-1.453152027 + t * 1.061405429)))
+    )
+    upper = 0.5 * poly * bell
+    phi = jnp.where(value >= 0.0, 1.0 - upper, upper)
+    return value * phi, phi + value * (bell * (2.0 * math.pi) ** -0.5)
+
+
+def feed_body(
+    tok, o_ref, x_ref, cot_ref, wp_ref, w1_ref, w2_ref, b1_ref, vec_ref,
+    out_ref, dmid_ref, datt_ref, gp_ref, g1_ref, g2_ref, gb1_ref, gvec_ref,
+    mid, h2, dm, y_acc, w1, w2, wp,
+):
+    step = pl.program_id(0)
+    last = pl.num_programs(0) - 1
+    part = 112
+    pieces = [slice(i * part, (i + 1) * part) for i in range(tok // part)]
+
+    @pl.when(step == 0)
+    def _():
+        for r in range(2):
+            for c in range(8):
+                p0, p1 = wp_ref[r * 16 + 2 * c], wp_ref[r * 16 + 2 * c + 1]
+                cols = slice(128 * c, 128 * c + 128)
+                wp[512 * r : 512 * r + 256, cols] = jnp.concatenate([p0[:, :64], p1[:, :64]], 1)
+                wp[512 * r + 256 : 512 * r + 512, cols] = jnp.concatenate([p0[:, 64:], p1[:, 64:]], 1)
+        mid[...] = lax.dot_general(o_ref[...], wp[...], TN, preferred_element_type=f32)
+        for rows in pieces:
+            total = x_ref[rows, :].astype(f32) + (mid[rows, :] + vec_ref[0:1, :])
+            mid[rows, :] = total
+            normed, _ = row_stats(total)
+            h2[rows, :] = (normed * vec_ref[1:2, :] + vec_ref[2:3, :]).astype(bf16)
+            dm[rows, :] = cot_ref[rows, :].astype(bf16)
+
+    for r in range(2):
+        for k in range(2):
+            for s in range(2):
+                w1[512 * r : 512 * r + 512, 256 * k + 128 * s : 256 * k + 128 * s + 128] = w1_ref[
+                    r, k, 512 * s : 512 * s + 512, :
+                ]
+    for c in range(8):
+        p0, p1 = w2_ref[0, 2 * c], w2_ref[0, 2 * c + 1]
+        cols = slice(128 * c, 128 * c + 128)
+        w2[0:256, cols] = jnp.concatenate([p0[:, :64], p1[:, :64]], 1)
+        w2[256:512, cols] = jnp.concatenate([p0[:, 64:], p1[:, 64:]], 1)
+
+    pre = jnp.dot(h2[...], w1[...], preferred_element_type=f32) + b1_ref[...]
+    act, slope = gelu_parts(pre)
+    act = act.astype(bf16)
+    dact = lax.dot_general(dm[...], w2[...], NT, preferred_element_type=f32)
+    dpre32 = dact * slope
+    dpre = dpre32.astype(bf16)
+    gb1_ref[...] = jnp.sum(dpre.astype(f32), axis=0, keepdims=True)
+    y = jnp.dot(act, w2[...], preferred_element_type=f32)
+    dh = lax.dot_general(dpre, w1[...], NT, preferred_element_type=f32)
+
+    @pl.when(step == 0)
+    def _():
+        y_acc[...] = y
+        dmid_ref[...] = dh
+
+    @pl.when(step > 0)
+    def _():
+        y_acc[...] += y
+        dmid_ref[...] += dh
+
+    g1 = lax.dot_general(h2[...], dpre, TN, preferred_element_type=f32).astype(bf16)
+    for r in range(2):
+        for k in range(2):
+            for s in range(2):
+                g1_ref[r, k, 512 * s : 512 * s + 512, :] = g1[
+                    512 * r : 512 * r + 512, 256 * k + 128 * s : 256 * k + 128 * s + 128
+                ]
+    g2 = lax.dot_general(act, dm[...], TN, preferred_element_type=f32).astype(bf16)
+    for c in range(8):
+        top = g2[0:256, 128 * c : 128 * c + 128]
+        low = g2[256:512, 128 * c : 128 * c + 128]
+        g2_ref[0, 2 * c] = jnp.concatenate([top[:, :64], low[:, :64]], 1)
+        g2_ref[0, 2 * c + 1] = jnp.concatenate([top[:, 64:], low[:, 64:]], 1)
+
+    @pl.when(step == last)
+    def _():
+        gain2 = vec_ref[1:2, :]
+        sums = [jnp.zeros((1, D), f32) for _ in range(4)]
+        for rows in pieces:
+            out_ref[rows, :] = (mid[rows, :] + (y_acc[rows, :] + vec_ref[3:4, :])).astype(bf16)
+            normed, inverse = row_stats(mid[rows, :])
+            e = dmid_ref[rows, :]
+            scaled = e * gain2
+            first = jnp.mean(scaled, axis=-1, keepdims=True)
+            second = jnp.mean(scaled * normed, axis=-1, keepdims=True)
+            grad = cot_ref[rows, :] + inverse * (scaled - first - normed * second)
+            dmid_ref[rows, :] = grad
+            branch = grad.astype(bf16)
+            h2[rows, :] = branch
+            for i, term in enumerate((e * normed, e, branch.astype(f32), dm[rows, :].astype(f32))):
+                sums[i] = sums[i] + jnp.sum(term, axis=0, keepdims=True)
+        gvec_ref[...] = jnp.concatenate(sums + [jnp.zeros((4, D), f32)], 0)
+        datt_ref[...] = lax.dot_general(h2[...], wp[...], NT, preferred_element_type=f32).astype(bf16)
+        gp = jnp.dot(o_ref[...], h2[...], preferred_element_type=f32).astype(bf16)
+        for r in range(2):
+            for c in range(8):
+                top = gp[512 * r : 512 * r + 256, 128 * c : 128 * c + 128]
+                low = gp[512 * r + 256 : 512 * r + 512, 128 * c : 128 * c + 128]
+                gp_ref[r * 16 + 2 * c] = jnp.concatenate([top[:, :64], low[:, :64]], 1)
+                gp_ref[r * 16 + 2 * c + 1] = jnp.concatenate([top[:, 64:], low[:, 64:]], 1)
+
+
+def feed_call(mixed, x_own, cot, gathered, bias1, vectors):
+    tok = x_own.shape[0]
+    by_block = gathered.reshape(2, 16, ROWS_B, 128)
+    zero2 = lambda j: (0, 0)
+    return pl.pallas_call(
+        lambda *refs: feed_body(tok, *refs),
+        out_shape=(
+            jax.ShapeDtypeStruct((tok, D), bf16),
+            jax.ShapeDtypeStruct((tok, D), f32),
+            jax.ShapeDtypeStruct((tok, D), bf16),
+            jax.ShapeDtypeStruct((32, ROWS_PROJ, 128), bf16),
+            jax.ShapeDtypeStruct((2, 16, ROWS_FC, 128), bf16),
+            jax.ShapeDtypeStruct((2, 16, ROWS_FC, 128), bf16),
+            jax.ShapeDtypeStruct((1, FF), f32),
+            jax.ShapeDtypeStruct((8, D), f32),
+        ),
+        grid=(8,),
+        in_specs=[
+            once((D, tok), zero2),
+            once((tok, D), zero2),
+            once((tok, D), zero2),
+            once((32, ROWS_PROJ, 128), lambda j: (0, 8, 0)),
+            pl.BlockSpec((2, 2, ROWS_FC, 128), lambda j: (0, j, 0, 0)),
+            pl.BlockSpec((1, 16, 256, 128), lambda j: (j // 4, 0, 4 + j % 4, 0)),
+            pl.BlockSpec((1, 512), lambda j: (0, j)),
+            once((8, D), zero2),
+        ],
+        out_specs=[
+            once((tok, D), zero2),
+            once((tok, D), zero2),
+            once((tok, D), zero2),
+            once((32, ROWS_PROJ, 128), lambda j: (0, 0, 0)),
+            pl.BlockSpec((2, 2, ROWS_FC, 128), lambda j: (0, j, 0, 0)),
+            pl.BlockSpec((1, 16, 256, 128), lambda j: (j // 4, 0, j % 4, 0)),
+            pl.BlockSpec((1, 512), lambda j: (0, j)),
+            once((8, D), zero2),
+        ],
+        scratch_shapes=[
+            pltpu.VMEM((tok, D), f32),
+            pltpu.VMEM((tok, D), bf16),
+            pltpu.VMEM((tok, D), bf16),
+            pltpu.VMEM((tok, D), f32),
+            pltpu.VMEM((D, 512), bf16),
+            pltpu.VMEM((512, D), bf16),
+            pltpu.VMEM((D, D), bf16),
+        ],
+        compiler_params=params(),
+        cost_estimate=cost(2 * tok * D * (6 * FF + 3 * D), 60e6, tok * FF * 2),
+        name="feed_forward_both",
+    )(mixed, x_own, cot, gathered, by_block, by_block, bias1, vectors)
+
+
+def project_back_body(tok, d0, d1, d2, x_own, x_oth, w00, w01, w10, w11, gain,
+                      own_ref, oth_ref, gbias_ref, gvec_ref, w_sc, acc):
+    step = pl.program_id(0)
+    assemble_qkv(((w00, w01), (w10, w11)), w_sc)
+    tile = jnp.concatenate([d0[...], d1[...], d2[...]], 1)
+    gbias_ref[...] = jnp.sum(tile.astype(f32), axis=0, keepdims=True)
+
+    @pl.when(step == 0)
+    def _():
+        acc[0:tok, :] = lax.dot_general(tile[0:tok], w_sc[...], NT, preferred_element_type=f32)
+        acc[tok : 2 * tok, :] = jnp.zeros((tok, D), f32)
+
+    @pl.when(step == 1)
+    def _():
+        acc[0:tok, :] += lax.dot_general(tile[0:tok], w_sc[...], NT, preferred_element_type=f32)
+
+    @pl.when(step >= 2)
+    def _():
+        acc[...] += lax.dot_general(tile, w_sc[...], NT, preferred_element_type=f32)
+
+    @pl.when(step == pl.num_programs(0) - 1)
+    def _():
+        first = jnp.zeros((1, D), f32)
+        second = jnp.zeros((1, D), f32)
+        for half, x_ref in enumerate((x_own, x_oth)):
+            for i in range(tok // 112):
+                rows = slice(i * 112, (i + 1) * 112)
+                e = acc[half * tok + i * 112 : half * tok + (i + 1) * 112, :]
+                normed, _ = row_stats(x_ref[rows, :].astype(f32))
+                first = first + jnp.sum(e * normed, axis=0, keepdims=True)
+                second = second + jnp.sum(e, axis=0, keepdims=True)
+                if half == 0:
+                    own_ref[rows, :] = e
+                else:
+                    oth_ref[rows, :] = e.astype(bf16)
+        gvec_ref[...] = jnp.concatenate([first, second, jnp.zeros((6, D), f32)], 0)
+
+
+def project_back_call(dqkv, x_own, x_oth, table, gathered, gain):
+    tok = x_own.shape[0]
+
+    def weight(r, k):
+        return pl.BlockSpec((1, ROWS_A, 128), lambda j, t: (t[r * 16 + 2 * j + k], 0, 0))
+
+    def piece(i):
+        return pl.BlockSpec((None, 2 * tok, 128), lambda j, t: ((3 * j + i) // 8, 0, (3 * j + i) % 8))
+
+    zero2 = lambda j, t: (0, 0)
+    return pl.pallas_call(
+        lambda t, *refs: project_back_body(tok, *refs),
+        out_shape=(
+            jax.ShapeDtypeStruct((tok, D), f32),
+            jax.ShapeDtypeStruct((tok, D), bf16),
+            jax.ShapeDtypeStruct((1, 3 * D), f32),
+            jax.ShapeDtypeStruct((8, D), f32),
+        ),
+        grid_spec=pltpu.PrefetchScalarGridSpec(
+            num_scalar_prefetch=1,
+            grid=(8,),
+            in_specs=[
+                piece(0),
+                piece(1),
+                piece(2),
+                once((tok, D), zero2),
+                once((tok, D), zero2),
+                weight(0, 0),
+                weight(0, 1),
+                weight(1, 0),
+                weight(1, 1),
+                once((1, D), zero2),
+            ],
+            out_specs=[
+                once((tok, D), zero2),
+                once((tok, D), zero2),
+                pl.BlockSpec((1, 384), lambda j, t: (0, j)),
+                once((8, D), zero2),
+            ],
+            scratch_shapes=[pltpu.VMEM((D, 384), bf16), pltpu.VMEM((2 * tok, D), f32)],
+        ),
+        compiler_params=params(),
+        cost_estimate=cost(2 * tok * D * D * 5, 24e6),
+        name="qkv_backward_tokens",
+    )(table, dqkv, dqkv, dqkv, x_own, x_oth, gathered, gathered, gathered, gathered, gain)
+
+
+def project_grad_body(tok, h_ref, d0, d1, d2, vec_ref, g_ref):
+    step = pl.program_id(0)
+
+    def write(rows):
+        tile = jnp.concatenate([d0[0:rows], d1[0:rows], d2[0:rows]], 1)
+        g = lax.dot_general(h_ref[0:rows, :], tile, TN, preferred_element_type=f32).astype(bf16)
+        for r in range(2):
+            lo, hi = g[512 * r : 512 * r + 256], g[512 * r + 256 : 512 * r + 512]
+            g_ref[r, 0, 0:256] = lo[:, 0:128]
+            g_ref[r, 0, 256:512] = hi[:, 0:128]
+            g_ref[r, 0, 512:768] = jnp.concatenate([lo[:, 128:192], hi[:, 128:192]], 1)
+            g_ref[r, 1, 0:256] = lo[:, 192:320]
+            g_ref[r, 1, 256:512] = hi[:, 192:320]
+            g_ref[r, 1, 512:768] = jnp.concatenate([lo[:, 320:384], hi[:, 320:384]], 1)
+
+    @pl.when(step < 2)
+    def _():
+        write(tok)
+
+    @pl.when(step >= 2)
+    def _():
+        write(2 * tok)
+
+    g_ref[:, :, 768:784] = vec_ref[...]
+
+
+def project_grad_call(hidden, dqkv, packed_vectors):
+    both = hidden.shape[0]
+    tok = both // 2
+
+    def piece(i):
+        return pl.BlockSpec((None, both, 128), lambda j: ((3 * j + i) // 8, 0, (3 * j + i) % 8))
+
+    return pl.pallas_call(
+        lambda *refs: project_grad_body(tok, *refs),
+        out_shape=jax.ShapeDtypeStruct((2, 16, ROWS_A, 128), bf16),
+        grid=(8,),
+        in_specs=[
+            once((both, D), lambda j: (0, 0)),
+            piece(0),
+            piece(1),
+            piece(2),
+            pl.BlockSpec((2, 2, 16, 128), lambda j: (0, j, 0, 0)),
+        ],
+        out_specs=pl.BlockSpec((2, 2, ROWS_A, 128), lambda j: (0, j, 0, 0)),
+        compiler_params=params(),
+        cost_estimate=cost(2 * tok * D * D * 5, 20e6),
+        name="qkv_backward_weights",
+    )(hidden, dqkv, dqkv, dqkv, packed_vectors)
+
+
+def finish_body(own_ref, recv_ref, dmid_ref, x_ref, gain, out_ref):
+    e = own_ref[...] + recv_ref[...].astype(f32)
+    normed, inverse = row_stats(x_ref[...].astype(f32))
+    scaled = e * gain[...]
+    first = jnp.mean(scaled, axis=-1, keepdims=True)
+    second = jnp.mean(scaled * normed, axis=-1, keepdims=True)
+    out_ref[...] = dmid_ref[...] + inverse * (scaled - first - normed * second)
+
+
+def finish_call(own, recv, dmid, x_own, gain):
+    tok = own.shape[0]
+    block = pl.BlockSpec((112, D), lambda i: (i, 0))
+    return pl.pallas_call(
+        finish_body,
+        out_shape=jax.ShapeDtypeStruct((tok, D), f32),
+        grid=(tok // 112,),
+        in_specs=[block, block, block, block, pl.BlockSpec((1, D), lambda i: (0, 0))],
+        out_specs=block,
+        compiler_params=params(),
+        cost_estimate=cost(tok * D * 20, 13e6),
+        name="first_norm_backward",
+    )(own, recv, dmid, x_own, gain)
+
+
+AXES = ("row", "col")
+
+
+def swap_rows(value):
+    return lax.ppermute(value, "row", [(0, 1), (1, 0)])
+
+
+def gather_blocks(rows):
+    return lax.all_gather(rows, AXES, axis=0, tiled=False)
+
+
+def scatter_blocks(blocks):
+    flat = blocks.reshape((-1,) + blocks.shape[-2:])
+    return lax.psum_scatter(flat, AXES, scatter_dimension=0, tiled=False)
+
+
+def fast_device(
+    tokens, w_qkv, w_proj, w_fc1, w_fc2, ln1_gain, ln1_bias, q_bias, v_bias,
+    proj_bias, ln2_gain, ln2_bias, fc1_bias, fc2_bias, cotangent,
+):
+    small = (ln1_gain, ln1_bias, q_bias, v_bias, proj_bias, ln2_gain, ln2_bias, fc2_bias)
+    vec_rows = jnp.concatenate(small + (fc1_bias,)).reshape(3, 128)
+    shard_a = jnp.concatenate([pack_qkv(w_qkv), jnp.pad(vec_rows, ((0, 13), (0, 0)))], axis=0)
+    shard_b = jnp.concatenate([pack_fc1(w_fc1), pack_fc2(w_fc2), pack_proj(w_proj)], axis=0)
+    x_oth = swap_rows(tokens)
+    full_a = gather_blocks(shard_a)
+    full_b = gather_blocks(shard_b)
+    table = jnp.arange(32, dtype=jnp.int32)
+    vecs = full_a[:, ROWS_QKV : ROWS_QKV + 3].reshape(2, 16, 384).transpose(1, 0, 2).reshape(32, 384)
+    vecs = vecs.astype(f32)
+    flat = vecs[:, :256].reshape(32, 8, 32).transpose(1, 0, 2).reshape(8, D)
+    bias1 = vecs[:, 256:].reshape(1, FF)
+    gain1, shift1, bias_q, bias_v = (flat[i : i + 1] for i in range(4))
+    qkv_bias = jnp.concatenate([bias_q, jnp.zeros_like(bias_q), bias_v], axis=1)
+    second = jnp.concatenate([flat[4:8], jnp.zeros((4, D), f32)], axis=0)
+
+    hidden, qkv = qkv_call(tokens, x_oth, table, full_a, gain1, shift1, qkv_bias)
+    mixed, logsum = attend_call(qkv, tokens.shape[0])
+    out, dmid, datt, grad_p, grad_1, grad_2, gb1, gvec2 = feed_call(
+        mixed, tokens, cotangent, full_b, bias1, second
+    )
+    rs_2 = scatter_blocks(grad_2)
+    rs_1 = scatter_blocks(grad_1)
+    rs_p = scatter_blocks(grad_p)
+    dqkv = attend_back_call(qkv, datt, mixed, logsum)
+    own, oth, gbias, gvec1 = project_back_call(dqkv, tokens, x_oth, table, full_a, gain1)
+    recv = swap_rows(oth)
+    sums = jnp.concatenate(
+        [gvec1[0:2], gbias[:, :D], gbias[:, 2 * D :], gvec2[2:3], gvec2[0:2], gvec2[3:4]], axis=0
+    )
+    lanes = sums.reshape(8, 16, 2, 32).transpose(2, 1, 0, 3).reshape(2, 16, 2, 128)
+    ff_lanes = gb1.reshape(16, 2, 1, 128).transpose(1, 0, 2, 3)
+    packed = jnp.concatenate([lanes, ff_lanes, jnp.zeros((2, 16, 13, 128), f32)], axis=2).astype(bf16)
+    rs_a = scatter_blocks(project_grad_call(hidden, dqkv, packed))
+    grad_inputs = finish_call(own, recv, dmid, tokens, gain1)
+    vec = rs_a[ROWS_QKV : ROWS_QKV + 3].reshape(384).astype(f32)
+    pieces = [vec[32 * i : 32 * i + 32] for i in range(8)]
+    return (
+        out,
+        grad_inputs,
+        unpack_qkv(rs_a).astype(f32),
+        unpack_proj(rs_p).astype(f32),
+        unpack_fc1(rs_1).astype(f32),
+        unpack_fc2(rs_2).astype(f32),
+        *pieces[:7],
+        vec[256:384],
+        pieces[7],
+    )
+
+
 def solution(mesh):
+    fast = dict(mesh.shape) == {"row": 2, "col": 16}
     return jax.shard_map(
-        per_device,
+        fast_device if fast else per_device,
         mesh=mesh,
         in_specs=(
             P(("col", "row"), None),

time: 1220 us -> 928 us (0.76)
  matrix products: 343 us -> 0 us
  Pallas kernels: 0 us -> 271 us
  blocking collectives: 264 us -> 0 us
  waiting for transfers between devices: 300 us -> 556 us
  other arithmetic: 133 us -> 7.01 us
  local copies, waits for them, and re-layouts: 131 us -> 71.5 us
  starting transfers between devices: 20.9 us -> 4.86 us
    dot_general x18 -> x0, matrix products: 343 us -> none  [the longest x1 56.6 us: clip_backward(): jnp.einsum('qhd,khd->hqk', grad_mixed, value_rows, preferred_element_type...]
    pallas_call x0 -> x7, Pallas kernels: none -> 271 us  [the longest x1 94.2 us: feed_call(): pl.pallas_call(lambda *refs: feed_body(tok, *refs), out_shape=(jax.ShapeD...]
    reduce_scatter x8 -> x4, waiting for transfers between devices: 213 us -> 374 us  [scatter_blocks(): return lax.psum_scatter(flat, AXES, scatter_dimension=0, tiled=False)]
    all_gather x4 -> x2, waiting for transfers between devices: 0.06 us -> 133 us  [gather_blocks(): return lax.all_gather(rows, AXES, axis=0, tiled=False)]
    all_gather x6 -> x0, blocking collectives: 132 us -> none  [the longest x1 55.4 us: per_device(): lax.all_gather(w_fc2, 'row', axis=0, tiled=True)]
    unnamed x4 -> x0, blocking collectives: 131 us -> none
    all_to_all x4 -> x0, waiting for transfers between devices: 85.8 us -> none  [the longest x1 65.6 us: per_device(): lax.all_to_all(grad_triple.reshape(col_rows, 3, 1, per_group), 'row', spl...]
    convert_element_type x24 -> x5, other arithmetic: 81 us -> 3.25 us  [the longest x1 0.85 us: fast_device(): vecs = vecs.astype(f32)]
  transfers between devices with their start and end apart: 16 -> 8, of which waited for: 9 -> 6; matrix products, arithmetic and copies ran while one was open for 27% -> 5% of each run, Pallas kernels for 0% -> 19%
where the time goes in v1:
time: 928 us; the launch traced here: 926 us
  waiting for transfers between devices  556 us (60%)
  Pallas kernels  271 us (29%)
  local copies, waits for them, and re-layouts  71.5 us (8%)
  between operations  14.4 us (2%)
    reduce_scatter x4, waiting for transfers between devices, scatter_blocks(): return lax.psum_scatter(flat, AXES, scatter_dimension=0, tiled=False)  374 us
    all_gather x2, waiting for transfers between devices, gather_blocks(): return lax.all_gather(rows, AXES, axis=0, tiled=False)  133 us
    pallas_call x1, Pallas kernels, feed_call(): pl.pallas_call(lambda *refs: feed_body(tok, *refs), out_shape=(jax.ShapeD...  94.2 us
    pallas_call x1, Pallas kernels, attend_back_call(): pl.pallas_call(lambda *refs: attend_back_body(tok, keys, chunk, *refs), o...  65.8 us
    ppermute x2, waiting for transfers between devices, swap_rows(): return lax.ppermute(value, 'row', [(0, 1), (1, 0)])  48.3 us
    pallas_call x1, Pallas kernels, attend_call(): pl.pallas_call(lambda *refs: attend_body(tok, keys, chunk, *refs), out_sh...  29.7 us
    pallas_call x1, Pallas kernels, qkv_call(): pl.pallas_call(lambda t, *refs: qkv_body(tok, *refs), out_shape=(jax.Shap...  27.1 us
    pallas_call x1, Pallas kernels, project_back_call(): pl.pallas_call(lambda t, *refs: project_back_body(tok, *refs), out_shape=...  26 us
  transfers between devices with their start and end apart: 8, of which 6 were waited for; matrix products, arithmetic and copies ran while one was open for 5% of the time, Pallas kernels for 19%

profile of v1, /device:TPU:0, one launch (start us, length us, event | category | flops | bytes accessed | tf_op | source)
XLA Modules:
  0.0 925.6 jit_solution(3643496521587036630)
XLA Ops:
  7.2 0.8 fusion.3
  8.1 0.9 slice.157
  9.4 6.1 concatenate.42
  16.3 1.0 fusion.2
  17.9 0.9 maximum_maximum_fusion
  18.9 3.1 collective-permute-start
  22.0 69.1 %all-gather.5.cloned.1.call-done = bf16[25088,128]{1,0:T(8,128)(2,1)} async-done(((bf16[784,128]{1,0:T(8,128)(2,1)}), bf16[25088,128]{1,0:T(8,128)(2,1)}) %all-gather.5.cloned.1.call-update) | async-done | bytes 6422544 | tf_op jit(solution)/shard_map/all_gather | solution.py:1053
  91.1 0.8 slice_convert_fusion.1
  96.4 27.1 %qkv_forward.1 = (bf16[1568,1024]{1,0:T(8,128)(2,1)}, bf16[3,1568,1024]{2,1,0:T(8,128)(2,1)}) custom-call(s32[32]{0:T(128)} %iota.5.t, bf16[784,1024]{1,0:T(8,128)(2,1)} %x_ref.1, bf16[784,1024]{1,0:T(8,128)(2,1)} %collective-permute-done.refs_1_.refs_4_, bf16[32,784,128]{2,1,0:T(8,128)(2,1)} %bitcast.44, bf16[32,784,128]{2,1,0:T(8,128)(2,1)} %bitcast.45, ...), custom_call_target="tpu_custom_call" | custom-call | flops 8220835840 | bytes 24000000 | tf_op jit(solution)/shard_map/qkv_forward/pallas_call | solution.py:513
  123.5 29.7 %attention_forward.1 = (bf16[1024,784]{1,0:T(8,128)(2,1)}, f32[16,1,784]{2,1,0:T(1,128)}) custom-call(bf16[3,1568,1024]{2,1,0:T(8,128)(2,1)} %get-tuple-element.31.refs_0_.refs_1_.refs_2_, bf16[3,1568,1024]{2,1,0:T(8,128)(2,1)} %get-tuple-element.31.refs_0_.refs_1_.refs_2_, bf16[3,1568,1024]{2,1,0:T(8,128)(2,1)} %get-tuple-element.31.refs_0_.refs_1_.refs_2_), custom_call_target="tpu_custom_call" | custom-call | flops 20141047808 | bytes 12000000 | tf_op jit(solution)/shard_map/attention_forward/pallas_call | solution.py:595
  153.2 64.0 %all-gather.7.cloned.1.call-done = bf16[73728,128]{0,1:T(8,128)(2,1)} async-done(((bf16[2304,128]{0,1:T(8,128)(2,1)}), bf16[73728,128]{0,1:T(8,128)(2,1)}) %all-gather.7.cloned.1.call-update) | async-done | bytes 18874384 | tf_op jit(solution)/shard_map/all_gather | solution.py:1053
  217.2 24.1 %copy.75 = bf16[73728,128]{1,0:T(8,128)(2,1)} copy(bf16[73728,128]{0,1:T(8,128)(2,1)} %all-gather.7.cloned.1.call-done) | data formatting | bytes 37748736 | tf_op jit(solution)/shard_map/all_gather | solution.py:1053
  241.2 94.2 %feed_forward_both.1 = (bf16[784,1024]{1,0:T(8,128)(2,1)}, f32[784,1024]{1,0:T(8,128)}, bf16[784,1024]{1,0:T(8,128)(2,1)}, bf16[32,256,128]{2,1,0:T(8,128)(2,1)}...) custom-call(bf16[1024,784]{1,0:T(8,128)(2,1)} %get-tuple-element.32., ...), custom_call_target="tpu_custom_call" | custom-call | flops 44392513536 | bytes 60000000 | tf_op jit(solution)/shard_map/feed_forward_both/pallas_call | solution.py:837
  335.5 65.8 %attention_backward.1.refs_0_.refs_1_.refs_2_.refs_3_ = bf16[3,1568,1024]{2,1,0:T(8,128)(2,1)} custom-call(bf16[3,1568,1024]{2,1,0:T(8,128)(2,1)} %get-tuple-element.31.refs_0_.refs_1_.refs_2_, bf16[3,1568,1024]{2,1,0:T(8,128)(2,1)} %get-tuple-element.31.refs_0_.refs_1_.refs_2_, bf16[3,1568,1024]{2,1,0:T(8,128)(2,1)} %get-tuple-element.31.refs_0_.refs_1_.refs_2_, ...), custom_call_target="tpu_custom_call" | custom-call | flops 40282095616 | bytes 24000000 | tf_op jit(solution)/shard_map/attention_backward/pallas_call | solution.py:694
  401.8 26.0 %qkv_backward_tokens.1 = (f32[784,1024]{1,0:T(8,128)}, bf16[784,1024]{1,0:T(8,128)(2,1)}, f32[1,3072]{1,0:T(1,128)}, f32[8,1024]{1,0:T(8,128)}) custom-call(s32[32]{0:T(128)} %iota.6.t, bf16[3,1568,1024]{2,1,0:T(8,128)(2,1)} %attention_backward.1.refs_0_.refs_1_.refs_2_.refs_3_, bf16[3,1568,1024]{2,1,0:T(8,128)(2,1)} %attention_backward.1.refs_0_.refs_1_.refs_2_.refs_3_, ...), custom_call_target="tpu_custom_call" | custom-call | flops 8220835840 | bytes 24000000 | tf_op jit(solution)/shard_map/qkv_backward_tokens/pallas_call | solution.py:933
  430.5 20.0 %qkv_backward_weights.1 = bf16[2,16,784,128]{3,2,1,0:T(8,128)(2,1)} custom-call(bf16[1568,1024]{1,0:T(8,128)(2,1)} %get-tuple-element.39.refs_0_, bf16[3,1568,1024]{2,1,0:T(8,128)(2,1)} %attention_backward.1.refs_0_.refs_1_.refs_2_.refs_3_, bf16[3,1568,1024]{2,1,0:T(8,128)(2,1)} %attention_backward.1.refs_0_.refs_1_.refs_2_.refs_3_, ...), custom_call_target="tpu_custom_call" | custom-call | flops 8220835840 | bytes 20000000 | tf_op jit(solution)/shard_map/qkv_backward_weights/pallas_call | solution.py:1003
  450.5 10.4 %copy.80 = bf16[32,784,128]{1,2,0:T(8,128)(2,1)} copy(bf16[32,784,128]{2,1,0:T(8,128)(2,1)} %bitcast.52) | data formatting | bytes 12845056 | tf_op jit(solution)/shard_map/reshape | solution.py:1057
  461.0 12.0 %copy.81 = bf16[32,1024,128]{1,2,0:T(8,128)(2,1)} copy(bf16[32,1024,128]{2,1,0:T(8,128)(2,1)} %bitcast.57) | data formatting | bytes 16777216 | tf_op jit(solution)/shard_map/reshape | solution.py:1057
  473.6 1.6 collective-permute-start.1
  475.2 48.3 %collective-permute-done.1.recv_ref = bf16[784,1024]{1,0:T(8,128)(2,1)S(1)} collective-permute-done((bf16[784,1024]{1,0:T(8,128)(2,1)}, bf16[784,1024]{1,0:T(8,128)(2,1)S(1)}, u32[]{:S(2)}, u32[]{:S(2)}) %collective-permute-start.1) | collective-permute-done | bytes 1605664 | tf_op jit(solution)/shard_map/ppermute | solution.py:1049
  523.4 1.1 copy-done.1
  524.6 8.7 first_norm_backward.1
  533.3 1.0 fusion.4
  535.1 84.3 %reduce-scatter.5.cloned.1.call-done = bf16[1,784,128]{1,2,0:T(8,128)(2,1)} async-done(((bf16[32,784,128]{1,2,0:T(8,128)(2,1)}), bf16[1,784,128]{1,2,0:T(8,128)(2,1)}) %reduce-scatter.5.cloned.1.call-update) | async-done | bytes 200720 | tf_op jit(solution)/shard_map/reduce_scatter | solution.py:1058
  620.9 0.8 slice_bitcast_fusion.3
  621.8 0.9 slice_bitcast_fusion.2
  624.1 144.1 %reduce-scatter.11.cloned.1.call-done = bf16[1,1024,128]{1,2,0:T(8,128)(2,1)} async-done(((bf16[32,1024,128]{1,2,0:T(8,128)(2,1)}), bf16[1,1024,128]{1,2,0:T(8,128)(2,1)}) %reduce-scatter.11.cloned.1.call-update) | async-done | bytes 262160 | tf_op jit(solution)/shard_map/reduce_scatter | solution.py:1058
  768.2 1.2 reshape.110
  769.8 1.2 reshape.108
  771.0 146.0 %reduce-scatter.9.cloned.1.call-done = bf16[1,1024,128]{2,1,0:T(8,128)(2,1)} async-done(((bf16[32,1024,128]{2,1,0:T(8,128)(2,1)}), bf16[1,1024,128]{2,1,0:T(8,128)(2,1)}) %reduce-scatter.9.cloned.1.call-update) | async-done | bytes 262160 | tf_op jit(solution)/shard_map/reduce_scatter | solution.py:1058
  917.0 1.0 slice_bitcast_fusion.1
  918.0 0.8 maximum_convert_fusion
  (78 shorter events, 14.2 us)
Async XLA Ops:
  7.2 10.4 %copy-start.2 = (bf16[2048,64]{0,1:T(8,128)(2,1)S(1)}, bf16[2048,64]{0,1:T(8,128)(2,1)}, u32[]{:S(2)}) copy-start(bf16[2048,64]{0,1:T(8,128)(2,1)} %param.19) | copy-start | bytes 786436
  7.2 10.7 %copy-start.3 = (bf16[512,64]{0,1:T(8,128)(2,1)S(1)}, bf16[512,64]{0,1:T(8,128)(2,1)}, u32[]{:S(2)}) copy-start(bf16[512,64]{0,1:T(8,128)(2,1)} %param.17) | copy-start | bytes 196612
  7.2 83.9 %all-gather.5.cloned.1.call-start = ((), (), s32[]{:S(2)}) async-start(), calls=%async_computation.8 | async-start | bytes 6623232 | tf_op jit(solution)/shard_map/all_gather | solution.py:1053
  16.3 200.9 %all-gather.7.cloned.1.call-start = ((), (), s32[]{:S(2)}) async-start(), calls=%async_computation.9 | async-start | bytes 19464192 | tf_op jit(solution)/shard_map/all_gather | solution.py:1053
  17.3 1.6 copy-start
  18.8 514.5 %reduce-scatter.7.cloned.1.call-start = ((), (), s32[]{:S(2)}) async-start(), calls=%async_computation.5 | async-start | bytes 2162688 | tf_op jit(solution)/shard_map/reduce_scatter | solution.py:1058
  18.9 77.0 %collective-permute-start = (bf16[784,1024]{1,0:T(8,128)(2,1)S(1)}, bf16[784,1024]{1,0:T(8,128)(2,1)}, u32[]{:S(2)}, u32[]{:S(2)}) collective-permute-start(bf16[784,1024]{1,0:T(8,128)(2,1)S(1)} %copy-done), channel_id=1, source_target_pairs={{0,16},{16,0},{1,17},{17,1},{2,18},{18,2},{3,19},{19,3},{4,20},{20... | collective-permute-start | bytes 4816904 | tf_op jit(solution)/shard_map/ppermute | solution.py:1049
  335.5 283.9 %reduce-scatter.5.cloned.1.call-start = ((), (), s32[]{:S(2)}) async-start(), calls=%async_computation.4 | async-start | bytes 7569408 | tf_op jit(solution)/shard_map/reduce_scatter | solution.py:1058
  401.8 26.7 %copy-start.4 = (f32[8,1024]{1,0:T(8,128)S(1)}, f32[8,1024]{1,0:T(8,128)}, u32[]{:S(2)}) copy-start(f32[8,1024]{1,0:T(8,128)} %get-tuple-element.42) | copy-start | bytes 98308
  401.8 27.8 %copy-start.5 = (f32[1,4096]{1,0:T(1,128)S(1)}, f32[1,4096]{1,0:T(1,128)}, u32[]{:S(2)}) copy-start(f32[1,4096]{1,0:T(1,128)} %get-tuple-element.43) | copy-start | bytes 49156
  461.0 307.2 %reduce-scatter.11.cloned.1.call-start = ((), (), s32[]{:S(2)}) async-start(), calls=%async_computation.7 | async-start | bytes 8650752 | tf_op jit(solution)/shard_map/reduce_scatter | solution.py:1058
  473.0 444.0 %reduce-scatter.9.cloned.1.call-start = ((), (), s32[]{:S(2)}) async-start(), calls=%async_computation.6 | async-start | bytes 8650752 | tf_op jit(solution)/shard_map/reduce_scatter | solution.py:1058
  473.6 49.8 %collective-permute-start.1 = (bf16[784,1024]{1,0:T(8,128)(2,1)}, bf16[784,1024]{1,0:T(8,128)(2,1)S(1)}, u32[]{:S(2)}, u32[]{:S(2)}) collective-permute-start(bf16[784,1024]{1,0:T(8,128)(2,1)} %get-tuple-element.37), channel_id=1, source_target_pairs={{0,16},{16,0},{1,17},{17,1},{2,18},{18,2},{3,19},{19,3},{4,20},{20... | collective-permute-start | bytes 4816904 | tf_op jit(solution)/shard_map/ppermute | solution.py:1049
  523.4 1.1 copy-start.1
Sparse Core Ops, SparseCore 0:
  16.4 74.7 all-gather.4
  94.6 122.4 all-gather.6
  335.6 136.7 reduce-scatter.6
  474.6 144.7 reduce-scatter.4
  621.5 146.6 reduce-scatter.10
  770.3 146.6 reduce-scatter.8

commit v2 on v1

--- a/solution.py
+++ b/solution.py
@@ -1,3 +1,4 @@
+import functools
 import math
 
 import jax
@@ -418,47 +419,104 @@
     return centred * inverse, inverse
 
 
-def pack_qkv(block):
-    tail = block[:, 128:]
-    return jnp.concatenate(
-        [block[:, :128], jnp.concatenate([tail[:256], tail[256:]], axis=1)], axis=0
-    )
-
-
-def unpack_qkv(rows):
-    tail = rows[512:768]
-    return jnp.concatenate(
-        [rows[:512], jnp.concatenate([tail[:, :64], tail[:, 64:]], axis=0)], axis=1
-    )
-
-
-def pack_proj(block):
-    return jnp.concatenate([block[:256], block[256:]], axis=1)
-
-
-def unpack_proj(rows):
-    return jnp.concatenate([rows[:, :64], rows[:, 64:]], axis=0)
-
-
-def pack_fc1(block):
-    return jnp.concatenate([block[:, :128], block[:, 128:]], axis=0)
-
-
-def unpack_fc1(rows):
-    return jnp.concatenate([rows[:512], rows[512:]], axis=1)
-
-
-def pack_fc2(block):
-    return block.reshape(4, 2, 256, 64).transpose(0, 2, 1, 3).reshape(1024, 128)
-
-
-def unpack_fc2(rows):
-    return rows.reshape(4, 256, 2, 64).transpose(0, 2, 1, 3).reshape(2048, 64)
-
-
-def assemble_qkv(w_refs, w_out):
+def pack_a_body(w_ref, vec_ref, out_ref):
+    w = w_ref[...]
+    out_ref[0:512] = w[:, :128]
+    out_ref[512:768] = jnp.concatenate([w[:256, 128:], w[256:, 128:]], 1)
+    out_ref[768:784] = vec_ref[...]
+
+
+def pack_a(w_qkv, vec_rows):
+    return pl.pallas_call(
+        pack_a_body,
+        out_shape=jax.ShapeDtypeStruct((ROWS_A, 128), bf16),
+        compiler_params=params(),
+        cost_estimate=cost(1e5, 5e5),
+        name="pack_first",
+    )(w_qkv, vec_rows)
+
+
+def pack_b_body(w1_ref, w2_ref, wp_ref, out_ref):
+    w1 = w1_ref[...]
+    out_ref[0:512] = w1[:, :128]
+    out_ref[512:1024] = w1[:, 128:]
+    for q in range(4):
+        top, low = w2_ref[512 * q : 512 * q + 256], w2_ref[512 * q + 256 : 512 * q + 512]
+        out_ref[1024 + 256 * q : 1280 + 256 * q] = jnp.concatenate([top, low], 1)
+    out_ref[2048:2304] = jnp.concatenate([wp_ref[0:256], wp_ref[256:512]], 1)
+
+
+def pack_b(w_fc1, w_fc2, w_proj):
+    return pl.pallas_call(
+        pack_b_body,
+        out_shape=jax.ShapeDtypeStruct((ROWS_B, 128), bf16),
+        compiler_params=params(),
+        cost_estimate=cost(1e5, 1.5e6),
+        name="pack_second",
+    )(w_fc1, w_fc2, w_proj)
+
+
+def total_of(refs):
+    total = refs[0][0].astype(f32)
+    for ref in refs[1:4]:
+        total = total + ref[0].astype(f32)
+    for ref in refs[4:]:
+        total = total + ref[...].astype(f32)
+    return total
+
+
+def finish_a_body(*refs):
+    total, outs = total_of(refs[:7]), refs[7:]
+    outs[0][:, 0:128] = total[0:512]
+    outs[0][0:256, 128:192] = total[512:768, :64]
+    outs[0][256:512, 128:192] = total[512:768, 64:]
+    for i in range(8):
+        row, lane = i // 4, 32 * (i % 4)
+        outs[1 + i][...] = total[768 + row : 769 + row, lane : lane + 32]
+    outs[9][...] = total[770:771]
+
+
+def finish_1_body(*refs):
+    total = total_of(refs[:7])
+    refs[7][:, 0:128] = total[0:512]
+    refs[7][:, 128:256] = total[512:1024]
+
+
+def finish_2_body(*refs):
+    total = total_of(refs[:7])
+    for q in range(4):
+        piece = total[256 * q : 256 * q + 256]
+        refs[7][512 * q : 512 * q + 256] = piece[:, :64]
+        refs[7][512 * q + 256 : 512 * q + 512] = piece[:, 64:]
+
+
+def finish_p_body(ref, out_ref):
+    piece = ref[...].astype(f32)
+    out_ref[0:256] = piece[:, :64]
+    out_ref[256:512] = piece[:, 64:]
+
+
+def finish_sum(body, terms, shapes, name):
+    rows = terms[-1].shape[0]
+    block = pl.BlockSpec((1, rows, 128), lambda i: (0, 0, 0))
+    single = pl.BlockSpec((rows, 128), lambda i: (0, 0))
+    return pl.pallas_call(
+        body,
+        out_shape=tuple(jax.ShapeDtypeStruct(shape, f32) for shape in shapes),
+        grid=(1,),
+        in_specs=[block] * 4 + [single] * 3,
+        out_specs=tuple(pl.BlockSpec(shape, lambda i: (0, 0)) for shape in shapes),
+        compiler_params=params(),
+        cost_estimate=cost(1e6, 3e6),
+        name=name,
+    )(*terms)
+
+
+def assemble_qkv(core, w_refs, w_out):
     for r in range(2):
-        w0, w1 = w_refs[r][0][0], w_refs[r][1][0]
+        mine, theirs = w_refs[r][0][0], w_refs[r][1][0]
+        w0 = jnp.where(core == 0, mine, theirs)
+        w1 = jnp.where(core == 0, theirs, mine)
         a0, b0 = w0[:512], w0[512:768]
         a1, b1 = w1[:512], w1[512:768]
         lo = slice(512 * r, 512 * r + 256)
@@ -470,7 +528,7 @@
         w_out[hi, 256:384] = jnp.concatenate([a1[256:, 64:], b1[:, 64:]], axis=1)
 
 
-def qkv_body(tok, x_own, x_oth, w00, w01, w10, w11, gain, shift, bias, h_ref, qkv_ref, w_sc):
+def qkv_body(tok, tab, x_own, x_oth, w00, w01, w10, w11, gain, shift, bias, h_ref, qkv_ref, w_sc):
     step = pl.program_id(0)
 
     @pl.when(step == 0)
@@ -483,7 +541,7 @@
                     normed * gain[...] + shift[...]
                 ).astype(bf16)
 
-    assemble_qkv(((w00, w01), (w10, w11)), w_sc)
+    assemble_qkv(tab[32], ((w00, w01), (w10, w11)), w_sc)
 
     def project(rows):
         out = jnp.dot(h_ref[0:rows, :], w_sc[...], preferred_element_type=f32) + bias[...]
@@ -504,14 +562,14 @@
         project(2 * tok)
 
 
-def qkv_call(x_own, x_oth, table, gathered, gain, shift, bias):
+def qkv_call(x_own, x_oth, table, mine, theirs, gain, shift, bias):
     tok = x_own.shape[0]
 
     def weight(r, k):
-        return pl.BlockSpec((1, ROWS_A, 128), lambda j, t: (t[r * 16 + 2 * j + k], 0, 0))
+        return pl.BlockSpec((1, ROWS_A, 128), lambda j, t: (t[k * 16 + r * 8 + j], 0, 0))
 
     return pl.pallas_call(
-        lambda t, *refs: qkv_body(tok, *refs),
+        functools.partial(qkv_body, tok),
         out_shape=(
             jax.ShapeDtypeStruct((2 * tok, D), bf16),
             jax.ShapeDtypeStruct((3, 2 * tok, D), bf16),
@@ -539,7 +597,7 @@
         compiler_params=params(),
         cost_estimate=cost(2 * tok * D * D * 5, 24e6),
         name="qkv_forward",
-    )(table, x_own, x_oth, gathered, gathered, gathered, gathered, gain, shift, bias)
+    )(table, x_own, x_oth, mine, theirs, mine, theirs, gain, shift, bias)
 
 
 def attend_body(tok, keys, chunk, q_ref, k_ref, v_ref, o_ref, l_ref, *scratch):
@@ -621,7 +679,8 @@
     )(qkv, qkv, qkv)
 
 
-def attend_back_body(tok, keys, chunk, q_ref, k_ref, v_ref, g_ref, o_ref, l_ref, out_ref, *scratch):
+def attend_back_body(tok, keys, chunk, q_ref, k_ref, v_ref, g_ref, o_ref, l_ref, *rest):
+    out_ref, *scratch = rest[-6:]
     qx, gx, q_t, g_t, dq_sc = scratch
     lane = lax.broadcasted_iota(jnp.int32, (1, 128), 1)
     row = lax.broadcasted_iota(jnp.int32, (128, 1), 0)
@@ -684,37 +743,45 @@
     out_ref[0, tok:keys, :] = jnp.zeros((keys - tok, 128), bf16)
 
 
-def attend_back_call(qkv, grad, mixed, logsum, chunk=224):
+def attend_back_call(qkv, grad, mixed, logsum, pieces=4, chunk=224):
     tok = grad.shape[0]
     keys = qkv.shape[1]
-
-    def column(part, rows):
-        return pl.BlockSpec((None, rows, 128), lambda g: (part, 0, g))
-
-    return pl.pallas_call(
-        lambda *refs: attend_back_body(tok, keys, chunk, *refs),
-        out_shape=jax.ShapeDtypeStruct((3, keys, D), bf16),
-        grid=(H // 2,),
-        in_specs=[
-            column(0, tok),
-            column(1, keys),
-            column(2, keys),
-            pl.BlockSpec((tok, 128), lambda g: (0, g)),
-            pl.BlockSpec((128, tok), lambda g: (g, 0)),
-            pl.BlockSpec((2, 1, tok), lambda g: (g, 0, 0)),
-        ],
-        out_specs=pl.BlockSpec((3, keys, 128), lambda g: (0, 0, g)),
-        scratch_shapes=[
-            pltpu.VMEM((tok, 256), bf16),
-            pltpu.VMEM((tok, 256), bf16),
-            pltpu.VMEM((128, tok), bf16),
-            pltpu.VMEM((128, tok), bf16),
-            pltpu.VMEM((tok, 128), f32),
-        ],
-        compiler_params=params(),
-        cost_estimate=cost(16 * 8 * tok * keys * 256, 24e6, 16 * tok * keys),
-        name="attention_backward",
-    )(qkv, qkv, qkv, grad, mixed, logsum)
+    count = H // 2 // pieces
+    out = None
+    for first in range(0, H // 2, count):
+
+        def column(part, rows, first=first):
+            return pl.BlockSpec((None, rows, 128), lambda g: (part, 0, first + g))
+
+        out = pl.pallas_call(
+            functools.partial(attend_back_body, tok, keys, chunk),
+            out_shape=jax.ShapeDtypeStruct((3, keys, D), bf16),
+            grid=(count,),
+            in_specs=[
+                column(0, tok),
+                column(1, keys),
+                column(2, keys),
+                pl.BlockSpec((tok, 128), lambda g, first=first: (0, first + g)),
+                pl.BlockSpec((128, tok), lambda g, first=first: (first + g, 0)),
+                pl.BlockSpec((2, 1, tok), lambda g, first=first: (first + g, 0, 0)),
+            ]
+            + ([] if out is None else [pl.BlockSpec(memory_space=pl.ANY)]),
+            out_specs=pl.BlockSpec((3, keys, 128), lambda g, first=first: (0, 0, first + g)),
+            scratch_shapes=[
+                pltpu.VMEM((tok, 256), bf16),
+                pltpu.VMEM((tok, 256), bf16),
+                pltpu.VMEM((128, tok), bf16),
+                pltpu.VMEM((128, tok), bf16),
+                pltpu.VMEM((tok, 128), f32),
+            ],
+            input_output_aliases={} if out is None else {6: 0},
+            compiler_params=params(),
+            cost_estimate=cost(
+                16 * 8 * tok * keys * 256 / pieces, 24e6 / pieces, 16 * tok * keys / pieces
+            ),
+            name="attention_backward",
+        )(qkv, qkv, qkv, grad, mixed, logsum, *(() if out is None else (out,)))
+    return out
 
 
 def gelu_parts(value):
@@ -731,16 +798,16 @@
 
 
 def feed_body(
-    tok, o_ref, x_ref, cot_ref, wp_ref, w1_ref, w2_ref, b1_ref, vec_ref,
-    out_ref, dmid_ref, datt_ref, gp_ref, g1_ref, g2_ref, gb1_ref, gvec_ref,
-    mid, h2, dm, y_acc, w1, w2, wp,
+    tok, tab, o_ref, x_ref, cot_ref, wp_ref, w1_ref, w2_ref, b1_ref, vec_ref,
+    out_ref, dmid_ref, datt_ref, gp_ref, m1_ref, t1_ref, m2_ref, t2_ref, gb1_ref, gvec_ref,
+    mid, h2, dm, y_acc, w1, w2, wp, dpre_sc, g2_sc,
 ):
-    step = pl.program_id(0)
+    step, inner = pl.program_id(0), pl.program_id(1)
     last = pl.num_programs(0) - 1
     part = 112
     pieces = [slice(i * part, (i + 1) * part) for i in range(tok // part)]
 
-    @pl.when(step == 0)
+    @pl.when((step == 0) & (inner == 0))
     def _():
         for r in range(2):
             for c in range(8):
@@ -756,53 +823,68 @@
             h2[rows, :] = (normed * vec_ref[1:2, :] + vec_ref[2:3, :]).astype(bf16)
             dm[rows, :] = cot_ref[rows, :].astype(bf16)
 
-    for r in range(2):
-        for k in range(2):
+    @pl.when(inner == 0)
+    def _():
+        for r in range(2):
+            for k in range(2):
+                for s in range(2):
+                    cols = slice(256 * k + 128 * s, 256 * k + 128 * s + 128)
+                    w1[512 * r : 512 * r + 512, cols] = w1_ref[r, k, 512 * s : 512 * s + 512, :]
+        for c in range(8):
+            p0, p1 = w2_ref[0, 2 * c], w2_ref[0, 2 * c + 1]
+            cols = slice(128 * c, 128 * c + 128)
+            w2[0:256, cols] = jnp.concatenate([p0[:, :64], p1[:, :64]], 1)
+            w2[256:512, cols] = jnp.concatenate([p0[:, 64:], p1[:, 64:]], 1)
+        pre = jnp.dot(h2[...], w1[...], preferred_element_type=f32) + b1_ref[...]
+        act, slope = gelu_parts(pre)
+        act = act.astype(bf16)
+        dact = lax.dot_general(dm[...], w2[...], NT, preferred_element_type=f32)
+        dpre = (dact * slope).astype(bf16)
+        dpre_sc[...] = dpre
+        gb1_ref[...] = jnp.sum(dpre.astype(f32), axis=0, keepdims=True)
+        y = jnp.dot(act, w2[...], preferred_element_type=f32)
+        dh = lax.dot_general(dpre, w1[...], NT, preferred_element_type=f32)
+
+        @pl.when(step == 0)
+        def _():
+            y_acc[...] = y
+            dmid_ref[...] = dh
+
+        @pl.when(step > 0)
+        def _():
+            y_acc[...] += y
+            dmid_ref[...] += dh
+
+        g2_sc[...] = lax.dot_general(act, dm[...], TN, preferred_element_type=f32).astype(bf16)
+
+    def grad_1(rows):
+        g1 = lax.dot_general(h2[:, rows], dpre_sc[...], TN, preferred_element_type=f32).astype(bf16)
+        for ref, swap in ((m1_ref, 0), (t1_ref, 1)):
             for s in range(2):
-                w1[512 * r : 512 * r + 512, 256 * k + 128 * s : 256 * k + 128 * s + 128] = w1_ref[
-                    r, k, 512 * s : 512 * s + 512, :
-                ]
-    for c in range(8):
-        p0, p1 = w2_ref[0, 2 * c], w2_ref[0, 2 * c + 1]
-        cols = slice(128 * c, 128 * c + 128)
-        w2[0:256, cols] = jnp.concatenate([p0[:, :64], p1[:, :64]], 1)
-        w2[256:512, cols] = jnp.concatenate([p0[:, 64:], p1[:, 64:]], 1)
-
-    pre = jnp.dot(h2[...], w1[...], preferred_element_type=f32) + b1_ref[...]
-    act, slope = gelu_parts(pre)
-    act = act.astype(bf16)
-    dact = lax.dot_general(dm[...], w2[...], NT, preferred_element_type=f32)
-    dpre32 = dact * slope
-    dpre = dpre32.astype(bf16)
-    gb1_ref[...] = jnp.sum(dpre.astype(f32), axis=0, keepdims=True)
-    y = jnp.dot(act, w2[...], preferred_element_type=f32)
-    dh = lax.dot_general(dpre, w1[...], NT, preferred_element_type=f32)
-
-    @pl.when(step == 0)
-    def _():
-        y_acc[...] = y
-        dmid_ref[...] = dh
-
-    @pl.when(step > 0)
-    def _():
-        y_acc[...] += y
-        dmid_ref[...] += dh
-
-    g1 = lax.dot_general(h2[...], dpre, TN, preferred_element_type=f32).astype(bf16)
-    for r in range(2):
-        for k in range(2):
-            for s in range(2):
-                g1_ref[r, k, 512 * s : 512 * s + 512, :] = g1[
-                    512 * r : 512 * r + 512, 256 * k + 128 * s : 256 * k + 128 * s + 128
-                ]
-    g2 = lax.dot_general(act, dm[...], TN, preferred_element_type=f32).astype(bf16)
-    for c in range(8):
-        top = g2[0:256, 128 * c : 128 * c + 128]
-        low = g2[256:512, 128 * c : 128 * c + 128]
-        g2_ref[0, 2 * c] = jnp.concatenate([top[:, :64], low[:, :64]], 1)
-        g2_ref[0, 2 * c + 1] = jnp.concatenate([top[:, 64:], low[:, 64:]], 1)
-
-    @pl.when(step == last)
+                ref[0, 0, 512 * s : 512 * s + 512, :] = jnp.where(
+                    tab[32] == swap,
+                    g1[:, 128 * s : 128 * s + 128],
+                    g1[:, 256 + 128 * s : 384 + 128 * s],
+                )
+
+    def grad_2(x):
+        for z in range(4):
+            cols = slice(128 * (2 * z + x), 128 * (2 * z + x) + 128)
+            top, low = g2_sc[0:256, cols], g2_sc[256:512, cols]
+            even = jnp.concatenate([top[:, :64], low[:, :64]], 1)
+            odd = jnp.concatenate([top[:, 64:], low[:, 64:]], 1)
+            at = tab[35 + z]
+            m2_ref[0, at] = jnp.where(tab[32] == 0, even, odd)
+            t2_ref[0, at] = jnp.where(tab[32] == 0, odd, even)
+
+    for i in range(2):
+
+        @pl.when(inner == i)
+        def _(i=i):
+            grad_1(slice(512 * i, 512 * i + 512))
+            grad_2(i)
+
+    @pl.when((step == last) & (inner == 1))
     def _():
         gain2 = vec_ref[1:2, :]
         sums = [jnp.zeros((1, D), f32) for _ in range(4)]
@@ -830,62 +912,85 @@
                 gp_ref[r * 16 + 2 * c + 1] = jnp.concatenate([top[:, 64:], low[:, 64:]], 1)
 
 
-def feed_call(mixed, x_own, cot, gathered, bias1, vectors):
+def feed_call(mixed, x_own, cot, table, gathered, bias1, vectors):
     tok = x_own.shape[0]
     by_block = gathered.reshape(2, 16, ROWS_B, 128)
-    zero2 = lambda j: (0, 0)
+    zero2 = lambda j, i, t: (0, 0)
+    zero3 = lambda j, i, t: (0, 0, 0)
+    blocks = jax.ShapeDtypeStruct((4, 4, ROWS_FC, 128), bf16)
+
+    def out_1(k):
+        return pl.BlockSpec(
+            (1, 1, ROWS_FC, 128),
+            lambda j, i, t: (t[k * 16 + i * 8 + j] // 4, t[k * 16 + i * 8 + j] % 4, 0, 0),
+        )
+
+    def out_2(k):
+        return pl.BlockSpec(
+            (1, 4, 256, 128), lambda j, i, t: (t[k * 16 + (j // 4) * 8 + i] // 4, 0, j % 4, 0)
+        )
+
     return pl.pallas_call(
-        lambda *refs: feed_body(tok, *refs),
+        functools.partial(feed_body, tok),
         out_shape=(
             jax.ShapeDtypeStruct((tok, D), bf16),
             jax.ShapeDtypeStruct((tok, D), f32),
             jax.ShapeDtypeStruct((tok, D), bf16),
             jax.ShapeDtypeStruct((32, ROWS_PROJ, 128), bf16),
-            jax.ShapeDtypeStruct((2, 16, ROWS_FC, 128), bf16),
-            jax.ShapeDtypeStruct((2, 16, ROWS_FC, 128), bf16),
+            blocks,
+            blocks,
+            blocks,
+            blocks,
             jax.ShapeDtypeStruct((1, FF), f32),
             jax.ShapeDtypeStruct((8, D), f32),
         ),
-        grid=(8,),
-        in_specs=[
-            once((D, tok), zero2),
-            once((tok, D), zero2),
-            once((tok, D), zero2),
-            once((32, ROWS_PROJ, 128), lambda j: (0, 8, 0)),
-            pl.BlockSpec((2, 2, ROWS_FC, 128), lambda j: (0, j, 0, 0)),
-            pl.BlockSpec((1, 16, 256, 128), lambda j: (j // 4, 0, 4 + j % 4, 0)),
-            pl.BlockSpec((1, 512), lambda j: (0, j)),
-            once((8, D), zero2),
-        ],
-        out_specs=[
-            once((tok, D), zero2),
-            once((tok, D), zero2),
-            once((tok, D), zero2),
-            once((32, ROWS_PROJ, 128), lambda j: (0, 0, 0)),
-            pl.BlockSpec((2, 2, ROWS_FC, 128), lambda j: (0, j, 0, 0)),
-            pl.BlockSpec((1, 16, 256, 128), lambda j: (j // 4, 0, j % 4, 0)),
-            pl.BlockSpec((1, 512), lambda j: (0, j)),
-            once((8, D), zero2),
-        ],
-        scratch_shapes=[
-            pltpu.VMEM((tok, D), f32),
-            pltpu.VMEM((tok, D), bf16),
-            pltpu.VMEM((tok, D), bf16),
-            pltpu.VMEM((tok, D), f32),
-            pltpu.VMEM((D, 512), bf16),
-            pltpu.VMEM((512, D), bf16),
-            pltpu.VMEM((D, D), bf16),
-        ],
+        grid_spec=pltpu.PrefetchScalarGridSpec(
+            num_scalar_prefetch=1,
+            grid=(8, 2),
+            in_specs=[
+                once((D, tok), zero2),
+                once((tok, D), zero2),
+                once((tok, D), zero2),
+                once((32, ROWS_PROJ, 128), lambda j, i, t: (0, 8, 0)),
+                pl.BlockSpec((2, 2, ROWS_FC, 128), lambda j, i, t: (0, j, 0, 0)),
+                pl.BlockSpec((1, 16, 256, 128), lambda j, i, t: (j // 4, 0, 4 + j % 4, 0)),
+                pl.BlockSpec((1, 512), lambda j, i, t: (0, j)),
+                once((8, D), zero2),
+            ],
+            out_specs=[
+                once((tok, D), zero2),
+                once((tok, D), zero2),
+                once((tok, D), zero2),
+                once((32, ROWS_PROJ, 128), zero3),
+                out_1(0),
+                out_1(1),
+                out_2(0),
+                out_2(1),
+                pl.BlockSpec((1, 512), lambda j, i, t: (0, j)),
+                once((8, D), zero2),
+            ],
+            scratch_shapes=[
+                pltpu.VMEM((tok, D), f32),
+                pltpu.VMEM((tok, D), bf16),
+                pltpu.VMEM((tok, D), bf16),
+                pltpu.VMEM((tok, D), f32),
+                pltpu.VMEM((D, 512), bf16),
+                pltpu.VMEM((512, D), bf16),
+                pltpu.VMEM((D, D), bf16),
+                pltpu.VMEM((tok, 512), bf16),
+                pltpu.VMEM((512, D), bf16),
+            ],
+        ),
         compiler_params=params(),
         cost_estimate=cost(2 * tok * D * (6 * FF + 3 * D), 60e6, tok * FF * 2),
         name="feed_forward_both",
-    )(mixed, x_own, cot, gathered, by_block, by_block, bias1, vectors)
-
-
-def project_back_body(tok, d0, d1, d2, x_own, x_oth, w00, w01, w10, w11, gain,
+    )(table, mixed, x_own, cot, gathered, by_block, by_block, bias1, vectors)
+
+
+def project_back_body(tok, tab, d0, d1, d2, x_own, x_oth, w00, w01, w10, w11, gain,
                       own_ref, oth_ref, gbias_ref, gvec_ref, w_sc, acc):
     step = pl.program_id(0)
-    assemble_qkv(((w00, w01), (w10, w11)), w_sc)
+    assemble_qkv(tab[32], ((w00, w01), (w10, w11)), w_sc)
     tile = jnp.concatenate([d0[...], d1[...], d2[...]], 1)
     gbias_ref[...] = jnp.sum(tile.astype(f32), axis=0, keepdims=True)
 
@@ -920,18 +1025,18 @@
         gvec_ref[...] = jnp.concatenate([first, second, jnp.zeros((6, D), f32)], 0)
 
 
-def project_back_call(dqkv, x_own, x_oth, table, gathered, gain):
+def project_back_call(dqkv, x_own, x_oth, table, mine, theirs, gain):
     tok = x_own.shape[0]
 
     def weight(r, k):
-        return pl.BlockSpec((1, ROWS_A, 128), lambda j, t: (t[r * 16 + 2 * j + k], 0, 0))
+        return pl.BlockSpec((1, ROWS_A, 128), lambda j, t: (t[k * 16 + r * 8 + j], 0, 0))
 
     def piece(i):
         return pl.BlockSpec((None, 2 * tok, 128), lambda j, t: ((3 * j + i) // 8, 0, (3 * j + i) % 8))
 
     zero2 = lambda j, t: (0, 0)
     return pl.pallas_call(
-        lambda t, *refs: project_back_body(tok, *refs),
+        functools.partial(project_back_body, tok),
         out_shape=(
             jax.ShapeDtypeStruct((tok, D), f32),
             jax.ShapeDtypeStruct((tok, D), bf16),
@@ -964,23 +1069,23 @@
         compiler_params=params(),
         cost_estimate=cost(2 * tok * D * D * 5, 24e6),
         name="qkv_backward_tokens",
-    )(table, dqkv, dqkv, dqkv, x_own, x_oth, gathered, gathered, gathered, gathered, gain)
-
-
-def project_grad_body(tok, h_ref, d0, d1, d2, vec_ref, g_ref):
+    )(table, dqkv, dqkv, dqkv, x_own, x_oth, mine, theirs, mine, theirs, gain)
+
+
+def project_grad_body(tok, tab, h_ref, d0, d1, d2, vec_ref, mine_ref, theirs_ref):
     step = pl.program_id(0)
 
     def write(rows):
         tile = jnp.concatenate([d0[0:rows], d1[0:rows], d2[0:rows]], 1)
         g = lax.dot_general(h_ref[0:rows, :], tile, TN, preferred_element_type=f32).astype(bf16)
-        for r in range(2):
-            lo, hi = g[512 * r : 512 * r + 256], g[512 * r + 256 : 512 * r + 512]
-            g_ref[r, 0, 0:256] = lo[:, 0:128]
-            g_ref[r, 0, 256:512] = hi[:, 0:128]
-            g_ref[r, 0, 512:768] = jnp.concatenate([lo[:, 128:192], hi[:, 128:192]], 1)
-            g_ref[r, 1, 0:256] = lo[:, 192:320]
-            g_ref[r, 1, 256:512] = hi[:, 192:320]
-            g_ref[r, 1, 512:768] = jnp.concatenate([lo[:, 320:384], hi[:, 320:384]], 1)
+        lo, hi = g[0:256], g[256:512]
+        first = (g[:, 0:128], jnp.concatenate([lo[:, 128:192], hi[:, 128:192]], 1))
+        second = (g[:, 192:320], jnp.concatenate([lo[:, 320:384], hi[:, 320:384]], 1))
+        for ref, swap in ((mine_ref, 0), (theirs_ref, 1)):
+            even = tab[32] == swap
+            ref[0, 0:512] = jnp.where(even, first[0], second[0])
+            ref[0, 512:768] = jnp.where(even, first[1], second[1])
+            ref[0, 768:784] = jnp.where(even, vec_ref[0, 0], vec_ref[0, 1])
 
     @pl.when(step < 2)
     def _():
@@ -990,32 +1095,38 @@
     def _():
         write(2 * tok)
 
-    g_ref[:, :, 768:784] = vec_ref[...]
-
-
-def project_grad_call(hidden, dqkv, packed_vectors):
+
+def project_grad_call(hidden, dqkv, table, packed_vectors):
     both = hidden.shape[0]
     tok = both // 2
 
     def piece(i):
-        return pl.BlockSpec((None, both, 128), lambda j: ((3 * j + i) // 8, 0, (3 * j + i) % 8))
+        return pl.BlockSpec(
+            (None, both, 128), lambda j, r, t: ((3 * j + i) // 8, 0, (3 * j + i) % 8)
+        )
+
+    def out(k):
+        return pl.BlockSpec((1, ROWS_A, 128), lambda j, r, t: (t[k * 16 + r * 8 + j], 0, 0))
 
     return pl.pallas_call(
-        lambda *refs: project_grad_body(tok, *refs),
-        out_shape=jax.ShapeDtypeStruct((2, 16, ROWS_A, 128), bf16),
-        grid=(8,),
-        in_specs=[
-            once((both, D), lambda j: (0, 0)),
-            piece(0),
-            piece(1),
-            piece(2),
-            pl.BlockSpec((2, 2, 16, 128), lambda j: (0, j, 0, 0)),
-        ],
-        out_specs=pl.BlockSpec((2, 2, ROWS_A, 128), lambda j: (0, j, 0, 0)),
+        functools.partial(project_grad_body, tok),
+        out_shape=(jax.ShapeDtypeStruct((16, ROWS_A, 128), bf16),) * 2,
+        grid_spec=pltpu.PrefetchScalarGridSpec(
+            num_scalar_prefetch=1,
+            grid=(8, 2),
+            in_specs=[
+                pl.BlockSpec((both, 512), lambda j, r, t: (0, r)),
+                piece(0),
+                piece(1),
+                piece(2),
+                pl.BlockSpec((1, 2, 16, 128), lambda j, r, t: (r, j, 0, 0)),
+            ],
+            out_specs=[out(0), out(1)],
+        ),
         compiler_params=params(),
         cost_estimate=cost(2 * tok * D * D * 5, 20e6),
         name="qkv_backward_weights",
-    )(hidden, dqkv, dqkv, dqkv, packed_vectors)
+    )(table, hidden, dqkv, dqkv, dqkv, packed_vectors)
 
 
 def finish_body(own_ref, recv_ref, dmid_ref, x_ref, gain, out_ref):
@@ -1045,17 +1156,73 @@
 AXES = ("row", "col")
 
 
+def spot(y, z, x, core):
+    return y * 16 + z * 4 + x * 2 + core
+
+
+def pairs_of(move):
+    return [
+        (spot(y, z, x, k), spot(*move(y, z, x, k)))
+        for y in range(2)
+        for z in range(4)
+        for x in range(2)
+        for k in range(2)
+    ]
+
+
+def along_z(d):
+    return pairs_of(lambda y, z, x, k: (y, z ^ d, x, k))
+
+
+SECOND = pairs_of(lambda y, z, x, k: (y, z, x ^ 1, k) if k == 0 else (y ^ 1, z, x, k))
+THIRD = pairs_of(lambda y, z, x, k: (y ^ 1, z, x, k) if k == 0 else (y, z, x ^ 1, k))
+CORE = pairs_of(lambda y, z, x, k: (y, z, x, k ^ 1))
+
+
+def send(value, pairs):
+    return lax.ppermute(value, AXES, pairs)
+
+
+def place_table():
+    y, c = lax.axis_index("row"), lax.axis_index("col")
+    z, x, core = c // 4, (c // 2) % 2, c % 2
+    index = jnp.arange(16, dtype=jnp.int32)
+    dy = (index // 8) ^ y
+    dx = (index % 2) ^ x
+    dz = ((index % 8) // 2) ^ z
+    even = dy * 8 + dx * 4 + dz
+    odd = dx * 8 + dy * 4 + dz
+    mine = jnp.where(core == 0, even, odd)
+    theirs = jnp.where(core == 0, odd, even)
+    rest = jnp.stack([core, y, c // 2]).astype(jnp.int32)
+    return jnp.concatenate([mine, theirs, rest, jnp.arange(4, dtype=jnp.int32) ^ z]).astype(jnp.int32)
+
+
+def gather_blocks(rows):
+    group = jnp.stack([rows] + [send(rows, along_z(d)) for d in (1, 2, 3)])
+    group = jnp.concatenate([group, send(group, SECOND)])
+    group = jnp.concatenate([group, send(group, THIRD)])
+    return group, send(group, CORE)
+
+
+def scatter_blocks(mine, theirs):
+    flat = (16,) + mine.shape[-2:]
+    mine, theirs = mine.reshape(flat), theirs.reshape(flat)
+
+    def part(arrays, where):
+        total = arrays[0][where].astype(f32)
+        for array in arrays[1:]:
+            total = total + array[where].astype(f32)
+        return total.astype(bf16)
+
+    arrays = [mine, send(theirs, CORE)]
+    arrays.append(send(part(arrays, slice(8, 16)), THIRD))
+    arrays.append(send(part(arrays, slice(4, 8)), SECOND))
+    return arrays + [send(part(arrays, d), along_z(d)) for d in (1, 2, 3)]
+
+
 def swap_rows(value):
     return lax.ppermute(value, "row", [(0, 1), (1, 0)])
-
-
-def gather_blocks(rows):
-    return lax.all_gather(rows, AXES, axis=0, tiled=False)
-
-
-def scatter_blocks(blocks):
-    flat = blocks.reshape((-1,) + blocks.shape[-2:])
-    return lax.psum_scatter(flat, AXES, scatter_dimension=0, tiled=False)
 
 
 def fast_device(
@@ -1064,30 +1231,32 @@
 ):
     small = (ln1_gain, ln1_bias, q_bias, v_bias, proj_bias, ln2_gain, ln2_bias, fc2_bias)
     vec_rows = jnp.concatenate(small + (fc1_bias,)).reshape(3, 128)
-    shard_a = jnp.concatenate([pack_qkv(w_qkv), jnp.pad(vec_rows, ((0, 13), (0, 0)))], axis=0)
-    shard_b = jnp.concatenate([pack_fc1(w_fc1), pack_fc2(w_fc2), pack_proj(w_proj)], axis=0)
+    table = place_table()
+    mine_a, theirs_a = gather_blocks(pack_a(w_qkv, jnp.pad(vec_rows, ((0, 13), (0, 0)))))
     x_oth = swap_rows(tokens)
-    full_a = gather_blocks(shard_a)
-    full_b = gather_blocks(shard_b)
-    table = jnp.arange(32, dtype=jnp.int32)
-    vecs = full_a[:, ROWS_QKV : ROWS_QKV + 3].reshape(2, 16, 384).transpose(1, 0, 2).reshape(32, 384)
-    vecs = vecs.astype(f32)
+    full_b = lax.all_gather(pack_b(w_fc1, w_fc2, w_proj), AXES, axis=0, tiled=False)
+    both = jnp.concatenate([mine_a[:, ROWS_QKV : ROWS_QKV + 3], theirs_a[:, ROWS_QKV : ROWS_QKV + 3]])
+    index = jnp.arange(32, dtype=jnp.int32)
+    core_of, row_of, chip_of = (index // 2) % 2, index % 2, index // 4
+    source = table[row_of * 8 + chip_of + 16 * (core_of != table[32])] + 16 * (core_of != table[32])
+    order = (source[:, None] == index[None, :]).astype(bf16)
+    vecs = jnp.dot(order, both.reshape(32, 384), preferred_element_type=f32)
     flat = vecs[:, :256].reshape(32, 8, 32).transpose(1, 0, 2).reshape(8, D)
     bias1 = vecs[:, 256:].reshape(1, FF)
     gain1, shift1, bias_q, bias_v = (flat[i : i + 1] for i in range(4))
     qkv_bias = jnp.concatenate([bias_q, jnp.zeros_like(bias_q), bias_v], axis=1)
     second = jnp.concatenate([flat[4:8], jnp.zeros((4, D), f32)], axis=0)
 
-    hidden, qkv = qkv_call(tokens, x_oth, table, full_a, gain1, shift1, qkv_bias)
+    hidden, qkv = qkv_call(tokens, x_oth, table, mine_a, theirs_a, gain1, shift1, qkv_bias)
     mixed, logsum = attend_call(qkv, tokens.shape[0])
-    out, dmid, datt, grad_p, grad_1, grad_2, gb1, gvec2 = feed_call(
-        mixed, tokens, cotangent, full_b, bias1, second
-    )
-    rs_2 = scatter_blocks(grad_2)
-    rs_1 = scatter_blocks(grad_1)
-    rs_p = scatter_blocks(grad_p)
+    out, dmid, datt, grad_p, mine_1, theirs_1, mine_2, theirs_2, gb1, gvec2 = feed_call(
+        mixed, tokens, cotangent, table, full_b, bias1, second
+    )
+    terms_2 = scatter_blocks(mine_2, theirs_2)
+    terms_1 = scatter_blocks(mine_1, theirs_1)
+    rs_p = lax.psum_scatter(grad_p, AXES, scatter_dimension=0, tiled=False)
     dqkv = attend_back_call(qkv, datt, mixed, logsum)
-    own, oth, gbias, gvec1 = project_back_call(dqkv, tokens, x_oth, table, full_a, gain1)
+    own, oth, gbias, gvec1 = project_back_call(dqkv, tokens, x_oth, table, mine_a, theirs_a, gain1)
     recv = swap_rows(oth)
     sums = jnp.concatenate(
         [gvec1[0:2], gbias[:, :D], gbias[:, 2 * D :], gvec2[2:3], gvec2[0:2], gvec2[3:4]], axis=0
@@ -1095,20 +1264,22 @@
     lanes = sums.reshape(8, 16, 2, 32).transpose(2, 1, 0, 3).reshape(2, 16, 2, 128)
     ff_lanes = gb1.reshape(16, 2, 1, 128).transpose(1, 0, 2, 3)
     packed = jnp.concatenate([lanes, ff_lanes, jnp.zeros((2, 16, 13, 128), f32)], axis=2).astype(bf16)
-    rs_a = scatter_blocks(project_grad_call(hidden, dqkv, packed))
+    terms_a = scatter_blocks(*project_grad_call(hidden, dqkv, table, packed))
     grad_inputs = finish_call(own, recv, dmid, tokens, gain1)
-    vec = rs_a[ROWS_QKV : ROWS_QKV + 3].reshape(384).astype(f32)
-    pieces = [vec[32 * i : 32 * i + 32] for i in range(8)]
+    (grad_fc1,) = finish_sum(finish_1_body, terms_1, [(512, 256)], "finish_fc1")
+    (grad_fc2,) = finish_sum(finish_2_body, terms_2, [(2048, 64)], "finish_fc2")
+    grad_proj = pl.pallas_call(
+        finish_p_body,
+        out_shape=jax.ShapeDtypeStruct((512, 64), f32),
+        compiler_params=params(),
+        name="finish_proj",
+    )(rs_p)
+    grad_qkv, *vec = finish_sum(
+        finish_a_body, terms_a, [(512, 192)] + [(1, 32)] * 8 + [(1, 128)], "finish_qkv"
+    )
+    vec = [value.reshape(-1) for value in vec]
     return (
-        out,
-        grad_inputs,
-        unpack_qkv(rs_a).astype(f32),
-        unpack_proj(rs_p).astype(f32),
-        unpack_fc1(rs_1).astype(f32),
-        unpack_fc2(rs_2).astype(f32),
-        *pieces[:7],
-        vec[256:384],
-        pieces[7],
+        out, grad_inputs, grad_qkv, grad_proj, grad_fc1, grad_fc2, *vec[:7], vec[8], vec[7],
     )
 
 

time: 928 us -> 668 us (0.72)
  the two profiles are of different devices: /device:TPU:0 before, /device:TPU:15 now
where the time goes in v2:
time: 668 us; the launch traced here: 663 us
  Pallas kernels  308 us (46%)
  waiting for transfers between devices  259 us (39%)
  local copies, waits for them, and re-layouts  33.3 us (5%)
  other arithmetic  25.3 us (4%)
  starting transfers between devices  22.2 us (3%)
  between operations  14.8 us (2%)
    ppermute x24, waiting for transfers between devices, send(): return lax.ppermute(value, AXES, pairs)  202 us
    pallas_call x1, Pallas kernels, feed_call(): pl.pallas_call(functools.partial(feed_body, tok), out_shape=(jax.ShapeDty...  101 us
    pallas_call x4, Pallas kernels, attend_back_call(): pl.pallas_call(functools.partial(attend_back_body, tok, keys, chunk), out...  73.9 us
    ppermute x2, waiting for transfers between devices, swap_rows(): return lax.ppermute(value, 'row', [(0, 1), (1, 0)])  56.7 us
    pallas_call x1, Pallas kernels, attend_call(): pl.pallas_call(lambda *refs: attend_body(tok, keys, chunk, *refs), out_sh...  29.6 us
    pallas_call x1, Pallas kernels, qkv_call(): pl.pallas_call(functools.partial(qkv_body, tok), out_shape=(jax.ShapeDtyp...  27.8 us
    pallas_call x1, Pallas kernels, project_grad_call(): pl.pallas_call(functools.partial(project_grad_body, tok), out_shape=(jax....  27.3 us
    pallas_call x1, Pallas kernels, project_back_call(): pl.pallas_call(functools.partial(project_back_body, tok), out_shape=(jax....  26.8 us
  transfers between devices with their start and end apart: 28, of which 14 were waited for; matrix products, arithmetic and copies ran while one was open for 7% of the time, Pallas kernels for 31%

profile of v2, /device:TPU:15, one launch (start us, length us, event | category | flops | bytes accessed | tf_op | source)
XLA Modules:
  0.0 663.3 jit_solution(6129189373089912166)
XLA Ops:
  19.1 4.5 collective-permute-done.1
  23.6 5.0 collective-permute-done.2
  28.6 15.5 %collective-permute-done.3 = bf16[784,128]{1,0:T(8,128)(2,1)S(1)} collective-permute-done((bf16[784,128]{1,0:T(8,128)(2,1)}, bf16[784,128]{1,0:T(8,128)(2,1)S(1)}, u32[]{:S(2)}, u32[]{:S(2)}) %collective-permute-start.3) | collective-permute-done | bytes 200736 | tf_op jit(solution)/shard_map/ppermute | solution.py:1183
  49.3 7.3 %collective-permute-done.4 = bf16[4,784,128]{2,1,0:T(8,128)(2,1)S(1)} collective-permute-done((bf16[4,784,128]{2,1,0:T(8,128)(2,1)S(1)}, bf16[4,784,128]{2,1,0:T(8,128)(2,1)S(1)}, u32[]{:S(2)}, u32[]{:S(2)}) %collective-permute-start.4) | collective-permute-done | bytes 802848 | tf_op jit(solution)/shard_map/ppermute | solution.py:1183
  57.9 39.4 %collective-permute-done.5 = bf16[8,784,128]{2,1,0:T(8,128)(2,1)S(1)} collective-permute-done((bf16[8,784,128]{2,1,0:T(8,128)(2,1)S(1)}, bf16[8,784,128]{2,1,0:T(8,128)(2,1)S(1)}, u32[]{:S(2)}, u32[]{:S(2)}) %collective-permute-start.5) | collective-permute-done | bytes 1605664 | tf_op jit(solution)/shard_map/ppermute | solution.py:1183
  98.5 2.5 collective-permute-start.6
  102.9 5.5 collective-permute-done.6.w01.w11
  113.0 56.7 %collective-permute-done.x_oth = bf16[784,1024]{1,0:T(8,128)(2,1)S(1)} collective-permute-done((bf16[784,1024]{1,0:T(8,128)(2,1)S(1)}, bf16[784,1024]{1,0:T(8,128)(2,1)S(1)}, u32[]{:S(2)}, u32[]{:S(2)}) %collective-permute-start) | collective-permute-done | bytes 1605664 | tf_op jit(solution)/shard_map/ppermute | solution.py:1225
  170.8 27.8 %qkv_forward.1 = (bf16[1568,1024]{1,0:T(8,128)(2,1)}, bf16[3,1568,1024]{2,1,0:T(8,128)(2,1)}) custom-call(s32[39]{0:T(128)} %copy-done, bf16[784,1024]{1,0:T(8,128)(2,1)} %x_ref.3, bf16[784,1024]{1,0:T(8,128)(2,1)} %copy-done.12, bf16[16,784,128]{2,1,0:T(8,128)(2,1)} %constant_dynamic-update-slice_fusion.5.w00.w10, ...), custom_call_target="tpu_custom_call" | custom-call | flops 8220835840 | bytes 24000000 | tf_op jit(solution)/shard_map/qkv_forward/pallas_call | solution.py:571
  198.7 29.6 %attention_forward.1 = (bf16[1024,784]{1,0:T(8,128)(2,1)}, f32[16,1,784]{2,1,0:T(1,128)}) custom-call(bf16[3,1568,1024]{2,1,0:T(8,128)(2,1)} %get-tuple-element.45.refs_0_.refs_1_.refs_2_.q_ref.k_ref.v_ref, bf16[3,1568,1024]{2,1,0:T(8,128)(2,1)} %get-tuple-element.45.refs_0_.refs_1_.refs_2_.q_ref.k_ref.v_ref, ...), custom_call_target="tpu_custom_call" | custom-call | flops 20141047808 | bytes 12000000 | tf_op jit(solution)/shard_map/attention_forward/pallas_call | solution.py:653
  228.2 101.2 %feed_forward_both.1 = (bf16[784,1024]{1,0:T(8,128)(2,1)}, f32[784,1024]{1,0:T(8,128)}, bf16[784,1024]{1,0:T(8,128)(2,1)}, bf16[32,256,128]{2,1,0:T(8,128)(2,1)}...) custom-call(s32[39]{0:T(128)} %copy-done, ...), custom_call_target="tpu_custom_call" | custom-call | flops 44392513536 | bytes 60000000 | tf_op jit(solution)/shard_map/feed_forward_both/pallas_call | solution.py:933
  332.4 18.3 %attention_backward.4.rest_0_ = bf16[3,1568,1024]{2,1,0:T(8,128)(2,1)} custom-call(bf16[3,1568,1024]{2,1,0:T(8,128)(2,1)} %get-tuple-element.45.refs_0_.refs_1_.refs_2_.q_ref.k_ref.v_ref, bf16[3,1568,1024]{2,1,0:T(8,128)(2,1)} %get-tuple-element.45.refs_0_.refs_1_.refs_2_.q_ref.k_ref.v_ref, ...), custom_call_target="tpu_custom_call" | custom-call | flops 10070523904 | bytes 6000000 | tf_op jit(solution)/shard_map/attention_backward/pallas_call | solution.py:756
  350.7 18.3 %attention_backward.5.rest_0_ = bf16[3,1568,1024]{2,1,0:T(8,128)(2,1)} custom-call(bf16[3,1568,1024]{2,1,0:T(8,128)(2,1)} %get-tuple-element.45.refs_0_.refs_1_.refs_2_.q_ref.k_ref.v_ref, bf16[3,1568,1024]{2,1,0:T(8,128)(2,1)} %get-tuple-element.45.refs_0_.refs_1_.refs_2_.q_ref.k_ref.v_ref, ...), custom_call_target="tpu_custom_call", output_to_operand_aliasing={{}: (6, {})} | custom-call | flops 10070523904 | bytes 6000000 | tf_op jit(solution)/shard_map/attention_backward/pallas_call | solution.py:756
  369.1 18.6 %attention_backward.6.rest_0_ = bf16[3,1568,1024]{2,1,0:T(8,128)(2,1)} custom-call(bf16[3,1568,1024]{2,1,0:T(8,128)(2,1)} %get-tuple-element.45.refs_0_.refs_1_.refs_2_.q_ref.k_ref.v_ref, bf16[3,1568,1024]{2,1,0:T(8,128)(2,1)} %get-tuple-element.45.refs_0_.refs_1_.refs_2_.q_ref.k_ref.v_ref, ...), custom_call_target="tpu_custom_call", output_to_operand_aliasing={{}: (6, {})} | custom-call | flops 10070523904 | bytes 6000000 | tf_op jit(solution)/shard_map/attention_backward/pallas_call | solution.py:756
  387.6 18.7 %attention_backward.7.d0.d1.d2 = bf16[3,1568,1024]{2,1,0:T(8,128)(2,1)} custom-call(bf16[3,1568,1024]{2,1,0:T(8,128)(2,1)} %get-tuple-element.45.refs_0_.refs_1_.refs_2_.q_ref.k_ref.v_ref, bf16[3,1568,1024]{2,1,0:T(8,128)(2,1)} %get-tuple-element.45.refs_0_.refs_1_.refs_2_.q_ref.k_ref.v_ref, ...), custom_call_target="tpu_custom_call", output_to_operand_aliasing={{}: (6, {})} | custom-call | flops 10070523904 | bytes 6000000 | tf_op jit(solution)/shard_map/attention_backward/pallas_call | solution.py:756
  406.4 26.8 %qkv_backward_tokens.1 = (f32[784,1024]{1,0:T(8,128)}, bf16[784,1024]{1,0:T(8,128)(2,1)}, f32[1,3072]{1,0:T(1,128)}, f32[8,1024]{1,0:T(8,128)}) custom-call(s32[39]{0:T(128)} %copy-done, bf16[3,1568,1024]{2,1,0:T(8,128)(2,1)} %attention_backward.7.d0.d1.d2, bf16[3,1568,1024]{2,1,0:T(8,128)(2,1)} %attention_backward.7.d0.d1.d2, ...), custom_call_target="tpu_custom_call" | custom-call | flops 8220835840 | bytes 24000000 | tf_op jit(solution)/shard_map/qkv_backward_tokens/pallas_call | solution.py:1038
  435.9 27.3 %qkv_backward_weights.1 = (bf16[16,784,128]{2,1,0:T(8,128)(2,1)}, bf16[16,784,128]{2,1,0:T(8,128)(2,1)}) custom-call(s32[39]{0:T(128)} %copy-done, bf16[1568,1024]{1,0:T(8,128)(2,1)} %get-tuple-element.53.h_ref, bf16[3,1568,1024]{2,1,0:T(8,128)(2,1)} %attention_backward.7.d0.d1.d2, bf16[3,1568,1024]{2,1,0:T(8,128)(2,1)} %attention_backward.7.d0.d1.d2, ...), custom_call_target="tpu_custom_call" | custom-call | flops 8220835840 | bytes 20000000 | tf_op jit(solution)/shard_map/qkv_backward_weights/pallas_call | solution.py:1111
  463.7 3.3 slice.277
  477.7 18.3 %collective-permute-done.9.refs_2_ = bf16[8,784,128]{2,1,0:T(8,128)(2,1)S(1)} collective-permute-done((bf16[8,784,128]{2,1,0:T(8,128)(2,1)S(1)}, bf16[8,784,128]{2,1,0:T(8,128)(2,1)S(1)}, u32[]{:S(2)}, u32[]{:S(2)}) %collective-permute-start.9) | collective-permute-done | bytes 1605664 | tf_op jit(solution)/shard_map/ppermute | solution.py:1183
  498.1 36.3 %collective-permute-done.21.refs_2_ = bf16[8,1024,128]{2,1,0:T(8,128)(2,1)S(1)} collective-permute-done((bf16[8,1024,128]{2,1,0:T(8,128)(2,1)S(1)}, bf16[8,1024,128]{2,1,0:T(8,128)(2,1)S(1)}, u32[]{:S(2)}, u32[]{:S(2)}) %collective-permute-start.21) | collective-permute-done | bytes 2097184 | tf_op jit(solution)/shard_map/ppermute | solution.py:1183
  534.4 2.7 fusion.3
  537.2 37.6 %collective-permute-done.15.refs_2_ = bf16[8,1024,128]{2,1,0:T(8,128)(2,1)S(1)} collective-permute-done((bf16[8,1024,128]{2,1,0:T(8,128)(2,1)S(1)}, bf16[8,1024,128]{2,1,0:T(8,128)(2,1)S(1)}, u32[]{:S(2)}, u32[]{:S(2)}) %collective-permute-start.15) | collective-permute-done | bytes 2097184 | tf_op jit(solution)/shard_map/ppermute | solution.py:1183
  574.8 2.7 fusion.5
  579.5 4.5 collective-permute-start.12
  584.0 3.0 fusion.11
  587.0 15.2 %collective-permute-done.16.refs_3_ = bf16[4,1024,128]{2,1,0:T(8,128)(2,1)S(1)} collective-permute-done((bf16[4,1024,128]{2,1,0:T(8,128)(2,1)S(1)}, bf16[4,1024,128]{2,1,0:T(8,128)(2,1)S(1)}, u32[]{:S(2)}, u32[]{:S(2)}) %collective-permute-start.16) | collective-permute-done | bytes 1048608 | tf_op jit(solution)/shard_map/ppermute | solution.py:1183
  602.2 2.9 fusion.8
  606.3 4.2 collective-permute-start.24
  614.0 8.6 %first_norm_backward.1 = f32[784,1024]{1,0:T(8,128)} custom-call(f32[784,1024]{1,0:T(8,128)} %get-tuple-element.50.own_ref, bf16[784,1024]{1,0:T(8,128)(2,1)} %copy-done.13, f32[784,1024]{1,0:T(8,128)} %get-tuple-element.52.dmid_ref, bf16[784,1024]{1,0:T(8,128)(2,1)} %x_ref.3, f32[1,1024]{1,0:T(1,128)} %slice.227.gain), custom_call_target="tpu_custom_call" | custom-call | flops 16056320 | bytes 13000000 | tf_op jit(solution)/shard_map/first_norm_backward/pallas_call | solution.py:1144
  630.4 12.8 %collective-permute-done.25.refs_6_ = bf16[1024,128]{1,0:T(8,128)(2,1)S(1)} collective-permute-done((bf16[1024,128]{1,0:T(8,128)(2,1)}, bf16[1024,128]{1,0:T(8,128)(2,1)S(1)}, u32[]{:S(2)}, u32[]{:S(2)}) %collective-permute-start.25) | collective-permute-done | bytes 262176 | tf_op jit(solution)/shard_map/ppermute | solution.py:1183
  643.9 2.7 finish_fc2.1
  649.0 4.1 collective-permute-done.19.refs_6_
  (182 shorter events, 66.5 us)
Async XLA Ops:
  7.3 221.0 %all-gather.3.cloned.1.call-start = ((), (), s32[]{:S(2)}) async-start(), calls=%async_computation.2 | async-start | bytes 19464192 | tf_op jit(solution)/shard_map/all_gather | solution.py:1237
  13.1 609.5 %reduce-scatter.2.cloned.1.call-start = ((), (), s32[]{:S(2)}) async-start(), calls=%async_computation.1 | async-start | bytes 2162688 | tf_op jit(solution)/shard_map/reduce_scatter | solution.py:1257
  16.5 7.1 %collective-permute-start.1 = (bf16[784,128]{1,0:T(8,128)(2,1)}, bf16[784,128]{1,0:T(8,128)(2,1)S(1)}, u32[]{:S(2)}, u32[]{:S(2)}) collective-permute-start(bf16[784,128]{1,0:T(8,128)(2,1)} %pack_first.1), channel_id=1, source_target_pairs={{0,4},{1,5},{2,6},{3,7},{4,0},{5,1},{6,2},{7,3},{8,12},{9,13},{10,... | collective-permute-start | bytes 602120 | tf_op jit(solution)/shard_map/ppermute | solution.py:1183
  16.6 12.0 %collective-permute-start.2 = (bf16[784,128]{1,0:T(8,128)(2,1)}, bf16[784,128]{1,0:T(8,128)(2,1)S(1)}, u32[]{:S(2)}, u32[]{:S(2)}) collective-permute-start(bf16[784,128]{1,0:T(8,128)(2,1)} %pack_first.1), channel_id=1, source_target_pairs={{0,8},{1,9},{2,10},{3,11},{4,12},{5,13},{6,14},{7,15},{8,0},{9,1},... | collective-permute-start | bytes 602120 | tf_op jit(solution)/shard_map/ppermute | solution.py:1183
  19.0 25.2 %collective-permute-start.3 = (bf16[784,128]{1,0:T(8,128)(2,1)}, bf16[784,128]{1,0:T(8,128)(2,1)S(1)}, u32[]{:S(2)}, u32[]{:S(2)}) collective-permute-start(bf16[784,128]{1,0:T(8,128)(2,1)} %pack_first.1), channel_id=1, source_target_pairs={{0,12},{1,13},{2,14},{3,15},{4,8},{5,9},{6,10},{7,11},{8,4},{9,5},... | collective-permute-start | bytes 602120 | tf_op jit(solution)/shard_map/ppermute | solution.py:1183
  45.2 11.4 %collective-permute-start.4 = (bf16[4,784,128]{2,1,0:T(8,128)(2,1)S(1)}, bf16[4,784,128]{2,1,0:T(8,128)(2,1)S(1)}, u32[]{:S(2)}, u32[]{:S(2)}) collective-permute-start(bf16[4,784,128]{2,1,0:T(8,128)(2,1)S(1)} %pad_maximum_fusion), channel_id=1, source_target_pairs={{0,2},{1,17},{2,0},{3,19},{4,6},{5,21},{6,4},{7,23},{8,10},{9,25},... | collective-permute-start | bytes 2408456 | tf_op jit(solution)/shard_map/ppermute | solution.py:1183
  48.6 52.5 %copy-start.7 = (bf16[784,1024]{1,0:T(8,128)(2,1)S(1)}, bf16[784,1024]{1,0:T(8,128)(2,1)}, u32[]{:S(2)}) copy-start(bf16[784,1024]{1,0:T(8,128)(2,1)} %x_ref.3) | copy-start | bytes 4816900
  57.7 39.6 %collective-permute-start.5 = (bf16[8,784,128]{2,1,0:T(8,128)(2,1)S(1)}, bf16[8,784,128]{2,1,0:T(8,128)(2,1)S(1)}, u32[]{:S(2)}, u32[]{:S(2)}) collective-permute-start(bf16[8,784,128]{2,1,0:T(8,128)(2,1)S(1)} %get-tuple-element.114), channel_id=1, source_target_pairs={{0,16},{1,3},{2,18},{3,1},{4,20},{5,7},{6,22},{7,5},{8,24},{9,11},... | collective-permute-start | bytes 4816904 | tf_op jit(solution)/shard_map/ppermute | solution.py:1183
  98.5 9.9 %collective-permute-start.6 = (bf16[16,784,128]{2,1,0:T(8,128)(2,1)}, bf16[16,784,128]{2,1,0:T(8,128)(2,1)}, u32[]{:S(2)}, u32[]{:S(2)}) collective-permute-start(bf16[16,784,128]{2,1,0:T(8,128)(2,1)} %constant_dynamic-update-slice_fusion.5.w00.w10), channel_id=1, source_target_pairs={{0,1},{1,0},{2,3},{3,2},{4,5},{5,4},{6,7},{7,6},{8,9},{9,8},{10,11... | collective-permute-start | bytes 9633800 | tf_op jit(solution)/shard_map/ppermute | solution.py:1183
  101.1 68.6 %collective-permute-start = (bf16[784,1024]{1,0:T(8,128)(2,1)S(1)}, bf16[784,1024]{1,0:T(8,128)(2,1)S(1)}, u32[]{:S(2)}, u32[]{:S(2)}) collective-permute-start(bf16[784,1024]{1,0:T(8,128)(2,1)S(1)} %copy-done.7), channel_id=1, source_target_pairs={{0,16},{16,0},{1,17},{17,1},{2,18},{18,2},{3,19},{19,3},{4,20},{20... | collective-permute-start | bytes 4816904 | tf_op jit(solution)/shard_map/ppermute | solution.py:1225
  101.3 68.4 %copy-start = (s32[39]{0:T(128)}, s32[39]{0:T(128)S(1)}, u32[]{:S(2)}) copy-start(s32[39]{0:T(128)S(1)} %concatenate.31.tab) | copy-start | bytes 472
  330.2 141.3 %collective-permute-start.20 = (bf16[16,1024,128]{2,1,0:T(8,128)(2,1)}, bf16[16,1024,128]{2,1,0:T(8,128)(2,1)}, u32[]{:S(2)}, u32[]{:S(2)}) collective-permute-start(bf16[16,1024,128]{2,1,0:T(8,128)(2,1)} %bitcast.104), channel_id=1, source_target_pairs={{0,1},{1,0},{2,3},{3,2},{4,5},{5,4},{6,7},{7,6},{8,9},{9,8},{10,11... | collective-permute-start | bytes 12582920 | tf_op jit(solution)/shard_map/ppermute | solution.py:1183
  332.3 142.9 %collective-permute-start.14 = (bf16[16,1024,128]{2,1,0:T(8,128)(2,1)}, bf16[16,1024,128]{2,1,0:T(8,128)(2,1)}, u32[]{:S(2)}, u32[]{:S(2)}) collective-permute-start(bf16[16,1024,128]{2,1,0:T(8,128)(2,1)} %bitcast.103), channel_id=1, source_target_pairs={{0,1},{1,0},{2,3},{3,2},{4,5},{5,4},{6,7},{7,6},{8,9},{9,8},{10,11... | collective-permute-start | bytes 12582920 | tf_op jit(solution)/shard_map/ppermute | solution.py:1183
  463.2 6.2 collective-permute-start.8
  471.5 24.5 %collective-permute-start.9 = (bf16[8,784,128]{2,1,0:T(8,128)(2,1)S(1)}, bf16[8,784,128]{2,1,0:T(8,128)(2,1)S(1)}, u32[]{:S(2)}, u32[]{:S(2)}) collective-permute-start(bf16[8,784,128]{2,1,0:T(8,128)(2,1)S(1)} %add_convert_fusion), channel_id=1, source_target_pairs={{0,16},{1,3},{2,18},{3,1},{4,20},{5,7},{6,22},{7,5},{8,24},{9,11},... | collective-permute-start | bytes 4816904 | tf_op jit(solution)/shard_map/ppermute | solution.py:1183
  473.8 60.6 %collective-permute-start.21 = (bf16[8,1024,128]{2,1,0:T(8,128)(2,1)S(1)}, bf16[8,1024,128]{2,1,0:T(8,128)(2,1)S(1)}, u32[]{:S(2)}, u32[]{:S(2)}) collective-permute-start(bf16[8,1024,128]{2,1,0:T(8,128)(2,1)S(1)} %fusion), channel_id=1, source_target_pairs={{0,16},{1,3},{2,18},{3,1},{4,20},{5,7},{6,22},{7,5},{8,24},{9,11},... | collective-permute-start | bytes 6291464 | tf_op jit(solution)/shard_map/ppermute | solution.py:1183
  477.4 97.4 %collective-permute-start.15 = (bf16[8,1024,128]{2,1,0:T(8,128)(2,1)S(1)}, bf16[8,1024,128]{2,1,0:T(8,128)(2,1)S(1)}, u32[]{:S(2)}, u32[]{:S(2)}) collective-permute-start(bf16[8,1024,128]{2,1,0:T(8,128)(2,1)S(1)} %fusion.1), channel_id=1, source_target_pairs={{0,16},{1,3},{2,18},{3,1},{4,20},{5,7},{6,22},{7,5},{8,24},{9,11},... | collective-permute-start | bytes 6291464 | tf_op jit(solution)/shard_map/ppermute | solution.py:1183
  477.7 127.4 %collective-permute-start.7 = (bf16[784,1024]{1,0:T(8,128)(2,1)S(1)}, bf16[784,1024]{1,0:T(8,128)(2,1)S(1)}, u32[]{:S(2)}, u32[]{:S(2)}) collective-permute-start(bf16[784,1024]{1,0:T(8,128)(2,1)S(1)} %copy-done.35), channel_id=1, source_target_pairs={{0,16},{16,0},{1,17},{17,1},{2,18},{18,2},{3,19},{19,3},{4,20},{20... | collective-permute-start | bytes 4816904 | tf_op jit(solution)/shard_map/ppermute | solution.py:1225
  496.0 81.6 %copy-start.8 = (bf16[8,784,128]{2,1,0:T(8,128)(2,1)}, bf16[8,784,128]{2,1,0:T(8,128)(2,1)S(1)}, u32[]{:S(2)}) copy-start(bf16[8,784,128]{2,1,0:T(8,128)(2,1)S(1)} %collective-permute-done.9.refs_2_) | copy-start | bytes 4816900
  498.0 79.6 %collective-permute-start.10 = (bf16[4,784,128]{2,1,0:T(8,128)(2,1)S(1)}, bf16[4,784,128]{2,1,0:T(8,128)(2,1)S(1)}, u32[]{:S(2)}, u32[]{:S(2)}) collective-permute-start(bf16[4,784,128]{2,1,0:T(8,128)(2,1)S(1)} %add_convert_fusion.1), channel_id=1, source_target_pairs={{0,2},{1,17},{2,0},{3,19},{4,6},{5,21},{6,4},{7,23},{8,10},{9,25},... | collective-permute-start | bytes 2408456 | tf_op jit(solution)/shard_map/ppermute | solution.py:1183
  534.4 49.6 %copy-start.6 = (bf16[8,1024,128]{2,1,0:T(8,128)(2,1)}, bf16[8,1024,128]{2,1,0:T(8,128)(2,1)S(1)}, u32[]{:S(2)}) copy-start(bf16[8,1024,128]{2,1,0:T(8,128)(2,1)S(1)} %collective-permute-done.21.refs_2_) | copy-start | bytes 6291460
  537.1 46.9 %collective-permute-start.22 = (bf16[4,1024,128]{2,1,0:T(8,128)(2,1)S(1)}, bf16[4,1024,128]{2,1,0:T(8,128)(2,1)S(1)}, u32[]{:S(2)}, u32[]{:S(2)}) collective-permute-start(bf16[4,1024,128]{2,1,0:T(8,128)(2,1)S(1)} %fusion.3), channel_id=1, source_target_pairs={{0,2},{1,17},{2,0},{3,19},{4,6},{5,21},{6,4},{7,23},{8,10},{9,25},... | collective-permute-start | bytes 3145736 | tf_op jit(solution)/shard_map/ppermute | solution.py:1183
  577.5 24.6 %collective-permute-start.16 = (bf16[4,1024,128]{2,1,0:T(8,128)(2,1)S(1)}, bf16[4,1024,128]{2,1,0:T(8,128)(2,1)S(1)}, u32[]{:S(2)}, u32[]{:S(2)}) collective-permute-start(bf16[4,1024,128]{2,1,0:T(8,128)(2,1)S(1)} %fusion.5), channel_id=1, source_target_pairs={{0,2},{1,17},{2,0},{3,19},{4,6},{5,21},{6,4},{7,23},{8,10},{9,25},... | collective-permute-start | bytes 3145736 | tf_op jit(solution)/shard_map/ppermute | solution.py:1183
  579.4 31.1 %collective-permute-start.11 = (bf16[784,128]{1,0:T(8,128)(2,1)S(1)}, bf16[784,128]{1,0:T(8,128)(2,1)S(1)}, u32[]{:S(2)}, u32[]{:S(2)}) collective-permute-start(bf16[784,128]{1,0:T(8,128)(2,1)S(1)} %get-tuple-element.113), channel_id=1, source_target_pairs={{0,4},{1,5},{2,6},{3,7},{4,0},{5,1},{6,2},{7,3},{8,12},{9,13},{10,... | collective-permute-start | bytes 602120 | tf_op jit(solution)/shard_map/ppermute | solution.py:1183
  579.5 31.1 %collective-permute-start.12 = (bf16[784,128]{1,0:T(8,128)(2,1)S(1)}, bf16[784,128]{1,0:T(8,128)(2,1)S(1)}, u32[]{:S(2)}, u32[]{:S(2)}) collective-permute-start(bf16[784,128]{1,0:T(8,128)(2,1)S(1)} %get-tuple-element.112), channel_id=1, source_target_pairs={{0,8},{1,9},{2,10},{3,11},{4,12},{5,13},{6,14},{7,15},{8,0},{9,1},... | collective-permute-start | bytes 602120 | tf_op jit(solution)/shard_map/ppermute | solution.py:1183
  584.0 27.8 %collective-permute-start.13 = (bf16[784,128]{1,0:T(8,128)(2,1)S(1)}, bf16[784,128]{1,0:T(8,128)(2,1)S(1)}, u32[]{:S(2)}, u32[]{:S(2)}) collective-permute-start(bf16[784,128]{1,0:T(8,128)(2,1)S(1)} %get-tuple-element.111), channel_id=1, source_target_pairs={{0,12},{1,13},{2,14},{3,15},{4,8},{5,9},{6,10},{7,11},{8,4},{9,5},... | collective-permute-start | bytes 602120 | tf_op jit(solution)/shard_map/ppermute | solution.py:1183
  602.2 11.5 %collective-permute-start.23 = (bf16[1024,128]{1,0:T(8,128)(2,1)S(1)}, bf16[1024,128]{1,0:T(8,128)(2,1)S(1)}, u32[]{:S(2)}, u32[]{:S(2)}) collective-permute-start(bf16[1024,128]{1,0:T(8,128)(2,1)S(1)} %get-tuple-element.107), channel_id=1, source_target_pairs={{0,4},{1,5},{2,6},{3,7},{4,0},{5,1},{6,2},{7,3},{8,12},{9,13},{10,... | collective-permute-start | bytes 786440 | tf_op jit(solution)/shard_map/ppermute | solution.py:1183
  606.3 24.1 %collective-permute-start.24 = (bf16[1024,128]{1,0:T(8,128)(2,1)}, bf16[1024,128]{1,0:T(8,128)(2,1)S(1)}, u32[]{:S(2)}, u32[]{:S(2)}) collective-permute-start(bf16[1024,128]{1,0:T(8,128)(2,1)} %get-tuple-element.106), channel_id=1, source_target_pairs={{0,8},{1,9},{2,10},{3,11},{4,12},{5,13},{6,14},{7,15},{8,0},{9,1},... | collective-permute-start | bytes 786440 | tf_op jit(solution)/shard_map/ppermute | solution.py:1183
  610.5 32.7 %collective-permute-start.25 = (bf16[1024,128]{1,0:T(8,128)(2,1)}, bf16[1024,128]{1,0:T(8,128)(2,1)S(1)}, u32[]{:S(2)}, u32[]{:S(2)}) collective-permute-start(bf16[1024,128]{1,0:T(8,128)(2,1)} %get-tuple-element.105), channel_id=1, source_target_pairs={{0,12},{1,13},{2,14},{3,15},{4,8},{5,9},{6,10},{7,11},{8,4},{9,5},... | collective-permute-start | bytes 786440 | tf_op jit(solution)/shard_map/ppermute | solution.py:1183
  611.2 37.8 %collective-permute-start.17 = (bf16[1024,128]{1,0:T(8,128)(2,1)}, bf16[1024,128]{1,0:T(8,128)(2,1)S(1)}, u32[]{:S(2)}, u32[]{:S(2)}) collective-permute-start(bf16[1024,128]{1,0:T(8,128)(2,1)} %get-tuple-element.110), channel_id=1, source_target_pairs={{0,4},{1,5},{2,6},{3,7},{4,0},{5,1},{6,2},{7,3},{8,12},{9,13},{10,... | collective-permute-start | bytes 786440 | tf_op jit(solution)/shard_map/ppermute | solution.py:1183
  611.9 37.1 %collective-permute-start.18 = (bf16[1024,128]{1,0:T(8,128)(2,1)}, bf16[1024,128]{1,0:T(8,128)(2,1)S(1)}, u32[]{:S(2)}, u32[]{:S(2)}) collective-permute-start(bf16[1024,128]{1,0:T(8,128)(2,1)} %get-tuple-element.109), channel_id=1, source_target_pairs={{0,8},{1,9},{2,10},{3,11},{4,12},{5,13},{6,14},{7,15},{8,0},{9,1},... | collective-permute-start | bytes 786440 | tf_op jit(solution)/shard_map/ppermute | solution.py:1183
  613.7 39.4 %collective-permute-start.19 = (bf16[1024,128]{1,0:T(8,128)(2,1)S(1)}, bf16[1024,128]{1,0:T(8,128)(2,1)S(1)}, u32[]{:S(2)}, u32[]{:S(2)}) collective-permute-start(bf16[1024,128]{1,0:T(8,128)(2,1)S(1)} %get-tuple-element.108), channel_id=1, source_target_pairs={{0,12},{1,13},{2,14},{3,15},{4,8},{5,9},{6,10},{7,11},{8,4},{9,5},... | collective-permute-start | bytes 786440 | tf_op jit(solution)/shard_map/ppermute | solution.py:1183
  (33 other events, 259.7 us)
Sparse Core Ops, SparseCore 0:
  13.2 175.8 all-gather.2
  468.5 124.6 reduce-scatter.1
